TPU v7x, 256 devices: a whole 4x4x8 slice. The times are simulated.
256 devices in a mesh: slab: 4 (over y_hi, core), hst: 64 (over y_lo, z, x).
Axes of the slice: x: 4, y: 4 (y_hi: 2, y_lo: 2; y = y_hi * 2 + y_lo), z: 8, core: 2. Of those that a mesh axis runs over, the one named last changes fastest.
Arguments:
- load: bfloat16 [288, 524288], P('slab', 'hst'), may hold values from -6 to 6
- host_rack: int32 [524288], P('hst'), may hold values from 0 to 16383, as said below
- rack_pod: int32 [16384], P('hst'), may hold values from 0 to 127
Outputs:
- host_drift: float32 [288, 524288], P('slab', 'hst')
- rack_drift: float32 [288, 16384], P('slab', 'hst')
- pod_drift: float32 [288, 128], P('slab', 'hst')
Inputs may be any that keep to these rules, and one draw needn't show every extreme that they name: `host_rack`: the hosts s * 8192 to (s + 1) * 8192 - 1 belong to racks among s * 256 to (s + 2) * 256 - 1, counted modulo 16384; racks hold uneven numbers of hosts, some none.
All inputs are finite; a program needn't handle non-finite values.
Results may differ from a plain program's by a relative error of at most 0.0003.
Values may be sent and summed in bfloat16 or wider, within the bound.
No kernel may reach another device: no remote copies, remote signals or barrier semaphores. Data moves between devices by JAX's collectives and lax.ppermute only.
A program may use at most 64 MiB of HBM per device.

v0:
```python
import math

import jax
import jax.numpy as jnp
from jax import lax
from jax.sharding import PartitionSpec as P

SLAB_LEN = 36
POD_DEV = 2


def carried_in(part, axis, combine, identity):
    place = lax.axis_index(axis)
    gathered = lax.all_gather(part, axis)
    state = jnp.zeros_like(part) + jnp.asarray(identity, part.dtype)

    def one(hop, state):
        return combine(state, lax.dynamic_index_in_dim(gathered, hop, 0, False))

    return lax.fori_loop(0, place, one, state)


def passed_along(value, axis, steps):
    count = lax.axis_size(axis)
    pairs = [(source, (source + steps) % count) for source in range(count)]
    return lax.ppermute(value, axis, pairs)


def with_halo(cells, sides, width):
    for axis, dim in sides:
        count = lax.axis_size(axis)
        head = lax.slice_in_dim(cells, 0, width, axis=dim)
        tail = lax.slice_in_dim(cells, cells.shape[dim] - width, cells.shape[dim], axis=dim)
        cells = jnp.concatenate(
            [
                lax.ppermute(tail, axis, [(i, (i + 1) % count) for i in range(count)]),
                cells,
                lax.ppermute(head, axis, [((i + 1) % count, i) for i in range(count)]),
            ],
            axis=dim,
        )
    return cells


def band_ones(step_rows, reach_steps, dtype):
    row_ids = lax.broadcasted_iota(jnp.int32, (step_rows, 3 * step_rows), 0)
    col_ids = lax.broadcasted_iota(jnp.int32, (step_rows, 3 * step_rows), 1)
    return (jnp.abs(col_ids - row_ids - step_rows) <= reach_steps).astype(dtype)


def lower_ones(step_rows):
    row_ids = lax.broadcasted_iota(jnp.int32, (step_rows, step_rows), 0)
    col_ids = lax.broadcasted_iota(jnp.int32, (step_rows, step_rows), 1)
    return (col_ids <= row_ids).astype(jnp.float32)


def local_prefix(series, extended, band, lower, window_size, precision):
    window_sums = jnp.dot(band, extended, preferred_element_type=jnp.float32, precision=precision)
    deviation = series.astype(jnp.float32) - window_sums / window_size
    return jnp.dot(
        lower, deviation, preferred_element_type=jnp.float32, precision=lax.Precision.HIGHEST
    )


def add_pair(earlier, later):
    return earlier + later


def slab_carry(totals):
    return carried_in(totals, "slab", add_pair, jnp.zeros_like(totals))


def rack_and_pod(series, local_rack, rack_pod):
    rack_count = rack_pod.shape[0]
    columns = lax.broadcasted_iota(jnp.int32, (1, 2 * rack_count), 1)
    member = (local_rack[:, None] == columns).astype(series.dtype)
    partial_sums = jnp.dot(series, member, preferred_element_type=jnp.float32, precision=None)
    arrived = passed_along(partial_sums[:, rack_count:], "hst", 1)
    rack_totals = partial_sums[:, :rack_count] + arrived
    pod_total = POD_DEV * lax.axis_size("hst")
    pod_columns = lax.broadcasted_iota(jnp.int32, (1, pod_total), 1)
    pod_member = (rack_pod[:, None] == pod_columns).astype(jnp.float32)
    pod_terms = jnp.dot(
        rack_totals, pod_member, preferred_element_type=jnp.float32, precision=lax.Precision.HIGHEST
    )
    pod_totals = lax.psum_scatter(pod_terms, "hst", scatter_dimension=1, tiled=True)
    return (rack_totals, pod_totals)


def on_device(load, host_rack, rack_pod):
    step_rows, hosts_here = load.shape
    rack_count = rack_pod.shape[0]
    total_racks = rack_count * lax.axis_size("hst")
    local_rack = (host_rack - lax.axis_index("hst") * rack_count) % total_racks
    reach_steps = 2 * SLAB_LEN
    window_size = 2 * reach_steps + 1
    day_steps = step_rows * lax.axis_size("slab")
    lower = lower_ones(step_rows)
    extended = with_halo(load, (("slab", 0),), step_rows)
    host_prefix = local_prefix(
        load, extended, band_ones(step_rows, reach_steps, jnp.bfloat16), lower, window_size, None
    )
    rack_load, pod_load = rack_and_pod(load, local_rack, rack_pod)
    groups = jnp.concatenate([rack_load, pod_load], 1)
    group_ext = with_halo(groups, (("slab", 0),), step_rows)
    group_prefix = local_prefix(
        groups,
        group_ext,
        band_ones(step_rows, reach_steps, jnp.float32),
        lower,
        window_size,
        lax.Precision.HIGHEST,
    )
    carried = slab_carry(jnp.concatenate([host_prefix[-1], group_prefix[-1]], 0))
    host_sum = host_prefix + carried[None, :hosts_here]
    group_sum = group_prefix + carried[None, hosts_here:]
    rack_sum = group_sum[:, :rack_count]
    pod_sum = group_sum[:, rack_count:]
    host_drift = host_sum * (1.0 / math.sqrt(day_steps))
    rack_drift = rack_sum * (1.0 / math.sqrt(day_steps * hosts_here / rack_count))
    pod_drift = pod_sum * (1.0 / math.sqrt(day_steps * hosts_here / POD_DEV))
    return (host_drift, rack_drift, pod_drift)


def solution(mesh):
    in_specs = (P("slab", "hst"), P("hst"), P("hst"))
    out_specs = (P("slab", "hst"), P("slab", "hst"), P("slab", "hst"))
    return jax.shard_map(
        on_device, mesh=mesh, in_specs=in_specs, out_specs=out_specs, check_vma=False
    )
```

profile of v0, /device:TPU:1, one launch (start us, length us, event | category | flops | bytes accessed | tf_op | source)
XLA Modules:
  0.0 391.4 jit_solution(7676802361590132499)
XLA Ops:
  7.2 0.0 all-reduce.4.cloned.1.call-start
  7.2 0.8 add_select_fusion
  8.0 0.0 copy-start.2
  8.0 0.0 copy-start.4
  8.0 0.0 copy-start.1
  8.0 0.0 copy-start.3
  8.0 4.1 %fusion.8 = f32[72,512]{1,0:T(8,128)S(1)} fusion(bf16[72,8192]{1,0:T(8,128)(2,1)} %param.5, s32[8192]{0:T(1024)S(1)} %add_select_fusion), kind=kOutput, calls=%fused_computation.12 | convolution fusion | flops 608174080 | bytes 1359872 | tf_op jit(solution)/shard_map/dot_general | solution.py:77
  12.2 2.1 collective-permute-start.2
  14.3 0.0 copy-done.2
  14.3 1.3 collective-permute-start.1
  15.6 2.5 collective-permute-start
  18.1 0.0 copy-done.4
  18.1 0.6 dynamic-slice.1
  19.3 4.4 %collective-permute-done.2 = f32[72,256]{1,0:T(8,128)S(1)} collective-permute-done((f32[72,256]{1,0:T(8,128)S(1)}, f32[72,256]{1,0:T(8,128)S(1)}, u32[]{:S(2)}, u32[]{:S(2)}) %collective-permute-start.2) | collective-permute-done | bytes 73760 | tf_op jit(solution)/shard_map/ppermute | solution.py:26
  23.7 0.0 copy-done.1
  23.7 0.3 fusion.17
  24.0 251.3 %all-reduce.1 = f32[72,128]{1,0:T(8,128)S(1)} all-reduce(f32[72,128]{1,0:T(8,128)S(1)} %fusion.17), channel_id=3, replica_groups=mesh['slab'=4,'hst'=64] {'hst'}, use_global_device_ids=true, to_apply=%region_0.1.clone | all-reduce | flops 9216 | bytes 73728
  275.3 0.1 constant_dynamic-slice_fusion
  275.4 55.2 %collective-permute-start.4 = (f32[72,258]{1,0:T(8,128)S(1)}, f32[72,258]{1,0:T(8,128)S(1)}, u32[]{:S(2)}, u32[]{:S(2)}) collective-permute-start(f32[72,258]{1,0:T(8,128)S(1)} %pad_maximum_fusion), channel_id=1, source_target_pairs={{64,0},{128,64},{192,128},{0,192},{65,1},{129,65},{193,129},{1,193... | collective-permute-start | bytes 222920 | tf_op jit(solution)/shard_map/ppermute | solution.py:38
  330.6 2.6 collective-permute-start.3
  333.2 0.0 copy-done.3
  333.2 0.6 dynamic-slice
  334.5 2.4 collective-permute-done.4
  336.9 0.0 collective-permute-done.3
  336.9 0.3 fusion.9
  337.2 0.2 fusion.23
  337.5 0.0 collective-permute-done.1
  337.5 0.0 collective-permute-done
  337.5 2.1 fusion.1
  339.6 1.4 fusion.24
  341.1 0.2 maximum_dynamic-update-slice_fusion
  341.3 0.0 copy-start
  341.3 0.6 copy-done
  342.0 0.0 all-reduce.4.cloned.1.call-update
  342.0 38.3 %all-reduce.4.cloned.1.call-done = f32[33800]{0:T(1024)} async-done(((f32[33800]{0:T(1024)}), f32[33800]{0:T(1024)}) %all-reduce.4.cloned.1.call-update) | async-done | bytes 135216
  380.3 1.0 reshape.10
  381.4 0.1 while.10
  381.4 0.1 dynamic-slice_reduce_fusion.2
  381.6 0.6 slice_multiply_fusion
  382.2 1.6 add_multiply_fusion
  383.9 0.6 copy.9
  (12 shorter events, 0.1 us)
Async XLA Ops:
  7.2 373.2 %all-reduce.4.cloned.1.call-start = ((), (), s32[]{:S(2)}) async-start(), calls=%async_computation | async-start | bytes 278528
  8.0 6.3 %copy-start.2 = (bf16[72,8192]{1,0:T(8,128)(2,1)S(1)}, bf16[72,8192]{1,0:T(8,128)(2,1)}, u32[]{:S(2)}) copy-start(bf16[72,8192]{1,0:T(8,128)(2,1)} %param.5) | copy-start | bytes 3538948
  8.0 10.1 %copy-start.4 = (u32[256]{0:T(256)S(1)}, u32[256]{0:T(256)}, u32[]{:S(2)}) copy-start(u32[256]{0:T(256)} %constant.60) | copy-start | bytes 3076
  8.0 15.7 %copy-start.1 = (s32[256]{0:T(256)S(1)}, s32[256]{0:T(256)}, u32[]{:S(2)}) copy-start(s32[256]{0:T(256)} %param.7) | copy-start | bytes 3076
  8.0 325.2 %copy-start.3 = (u32[256]{0:T(256)S(1)}, u32[256]{0:T(256)}, u32[]{:S(2)}) copy-start(u32[256]{0:T(256)} %constant.54) | copy-start | bytes 3076
  12.2 11.5 %collective-permute-start.2 = (f32[72,256]{1,0:T(8,128)S(1)}, f32[72,256]{1,0:T(8,128)S(1)}, u32[]{:S(2)}, u32[]{:S(2)}) collective-permute-start(f32[72,256]{1,0:T(8,128)S(1)} %slice.34), channel_id=1, source_target_pairs={{0,1},{1,2},{2,3},{3,4},{4,5},{5,6},{6,7},{7,8},{8,9},{9,10},{10,1... | collective-permute-start | bytes 221192 | tf_op jit(solution)/shard_map/ppermute | solution.py:26
  14.3 323.2 %collective-permute-start.1 = (bf16[72,8192]{1,0:T(8,128)(2,1)S(1)}, bf16[72,8192]{1,0:T(8,128)(2,1)S(1)}, u32[]{:S(2)}, u32[]{:S(2)}) collective-permute-start(bf16[72,8192]{1,0:T(8,128)(2,1)S(1)} %copy-done.2), channel_id=1, source_target_pairs={{64,0},{128,64},{192,128},{0,192},{65,1},{129,65},{193,129},{1,193... | collective-permute-start | bytes 3538952 | tf_op jit(solution)/shard_map/ppermute | solution.py:38
  15.6 321.9 %collective-permute-start = (bf16[72,8192]{1,0:T(8,128)(2,1)S(1)}, bf16[72,8192]{1,0:T(8,128)(2,1)}, u32[]{:S(2)}, u32[]{:S(2)}) collective-permute-start(bf16[72,8192]{1,0:T(8,128)(2,1)S(1)} %copy-done.2), channel_id=1, source_target_pairs={{0,64},{64,128},{128,192},{192,0},{1,65},{65,129},{129,193},{193,1... | collective-permute-start | bytes 3538952 | tf_op jit(solution)/shard_map/ppermute | solution.py:36
  275.4 61.5 %collective-permute-start.4 = (f32[72,258]{1,0:T(8,128)S(1)}, f32[72,258]{1,0:T(8,128)S(1)}, u32[]{:S(2)}, u32[]{:S(2)}) collective-permute-start(f32[72,258]{1,0:T(8,128)S(1)} %pad_maximum_fusion), channel_id=1, source_target_pairs={{64,0},{128,64},{192,128},{0,192},{65,1},{129,65},{193,129},{1,193... | collective-permute-start | bytes 222920 | tf_op jit(solution)/shard_map/ppermute | solution.py:38
  330.6 6.3 %collective-permute-start.3 = (f32[72,258]{1,0:T(8,128)S(1)}, f32[72,258]{1,0:T(8,128)S(1)}, u32[]{:S(2)}, u32[]{:S(2)}) collective-permute-start(f32[72,258]{1,0:T(8,128)S(1)} %pad_maximum_fusion), channel_id=1, source_target_pairs={{0,64},{64,128},{128,192},{192,0},{1,65},{65,129},{129,193},{193,1... | collective-permute-start | bytes 222920 | tf_op jit(solution)/shard_map/ppermute | solution.py:36
  341.3 0.7 copy-start
Sparse Core Ops, SparseCore 0:
  342.1 38.1 all-reduce.3
where the time goes:
time: 392 us; the launch traced here: 391 us
  blocking collectives  251 us (64%)
  starting transfers between devices  63.7 us (16%)
  waiting for transfers between devices  45.2 us (12%)
  between operations  15.5 us (4%)
  matrix products  8.4 us (2%)
    unnamed x1, blocking collectives  251 us
    ppermute x2, starting transfers between devices, with_halo(): lax.ppermute(head, axis, [((i + 1) % count, i) for i in range(count)])  56.5 us
    unnamed x2, waiting for transfers between devices  38.3 us
  transfers between devices with their start and end apart: 6, of which 3 were waited for; matrix products, arithmetic and copies ran while one was open for 1% of the time, Pallas kernels for 0%

commit v1 on v0

v1 whole, which is shorter than its diff:
```python
import math

import jax
import jax.numpy as jnp
from jax import lax
from jax.sharding import Mesh, PartitionSpec as P

SLAB_LEN = 36
POD_DEV = 2
SLAB = ("y_hi", "core")
HOST = ("y_lo", "z", "x")
ROW = ("z", "x")
HIGHEST = lax.Precision.HIGHEST


def ring(value, axes, steps):
    count = lax.axis_size(axes)
    return lax.ppermute(value, axes, [(i, (i + steps) % count) for i in range(count)])


def overlap(last, low, high):
    return jnp.maximum(jnp.minimum(last, high) - jnp.maximum(low, 0) + 1, 0)


def weights(out_step, in_step, day, reach):
    seen = jnp.zeros_like(out_step + in_step)
    for turn in (-day, 0, day):
        seen += overlap(out_step, in_step + turn - reach, in_step + turn + reach)
    return jnp.where(in_step <= out_step, 2 * reach + 1, 0) - seen


def on_device(load, host_rack, rack_pod):
    rows, hosts_here = load.shape
    rack_count = rack_pod.shape[0]
    slabs = lax.axis_size(SLAB)
    shards = lax.axis_size(HOST)
    row_size = lax.axis_size(ROW)
    lines = lax.axis_size("y_lo")
    total_racks = rack_count * shards
    day = rows * slabs
    reach = 2 * SLAB_LEN
    window = 2 * reach + 1
    slab = lax.axis_index(SLAB)
    bf16, f32, i32 = jnp.bfloat16, jnp.float32, jnp.int32

    before = ring(load, SLAB, 1)
    after = ring(load, SLAB, -1)
    next_pod = ring(rack_pod, HOST, -1)

    far = (slab + slabs // 2) % slabs
    steps = lax.broadcasted_iota(i32, (1, rows), 1)
    far_weights = weights(jnp.full((1, 1), far * rows, i32), slab * rows + steps, day, reach)
    far_row = jnp.dot(far_weights.astype(bf16), load, preferred_element_type=f32)
    far_row = lax.ppermute(far_row, SLAB, [(i, (i + slabs // 2) % slabs) for i in range(slabs)])

    local_rack = (host_rack - lax.axis_index(HOST) * rack_count) % total_racks
    columns = lax.broadcasted_iota(i32, (1, 2 * rack_count), 1)
    member = (local_rack[:, None] == columns).astype(bf16)
    part = jnp.dot(load, member, preferred_element_type=f32)
    shifted = ring(part[:, rack_count:], HOST, 1)

    pod_total = POD_DEV * shards
    mine = lines * POD_DEV
    place = lax.broadcasted_iota(i32, (pod_total, 1), 0)
    pod_id = (place % mine) // POD_DEV * (row_size * POD_DEV) + place // mine * POD_DEV + place % POD_DEV
    both = jnp.concatenate([rack_pod, next_pod])
    pod_member = (pod_id == both[None, :]).astype(f32)
    pod_part = lax.dot_general(
        pod_member, part, (((1,), (1,)), ((), ())), precision=HIGHEST, preferred_element_type=f32
    )
    pod_part = lax.all_to_all(pod_part, ROW, 0, 0, tiled=True)
    pod_part = jnp.sum(pod_part.reshape(row_size, mine, rows), 0)

    racks = part[:, :rack_count] + shifted
    racks_before = ring(racks, SLAB, 1)
    racks_after = ring(racks, SLAB, -1)
    racks_far = jnp.dot(far_weights.astype(f32), racks, precision=HIGHEST)

    spare = -(-rack_count // rows)
    packed = jnp.pad(racks_far.reshape(-1), (0, spare * rows - rack_count)).reshape(spare, rows)
    sent = jnp.concatenate([pod_part, packed], 0)
    got = lax.all_gather(sent, SLAB + ("y_lo",)).reshape(slabs, lines, mine + spare, rows)
    line = lax.axis_index("y_lo")
    pods = jnp.sum(lax.dynamic_slice_in_dim(got, line * POD_DEV, POD_DEV, 2), 1)
    rack_row = lax.dynamic_index_in_dim(got, far, 0, False)
    rack_row = lax.dynamic_index_in_dim(rack_row, line, 0, False)[mine:].reshape(-1)[:rack_count]

    out_step = slab * rows + lax.broadcasted_iota(i32, (rows, 1), 0)
    near = (slab - 1) * rows + lax.broadcasted_iota(i32, (1, 3 * rows), 1)
    near_weights = weights(out_step, (near + day) % day, day, reach)
    all_weights = weights(out_step, lax.broadcasted_iota(i32, (1, day), 1), day, reach)

    near_load = jnp.concatenate([before, load, after], 0)
    host_sum = jnp.dot(near_weights.astype(bf16), near_load, preferred_element_type=f32) + far_row
    near_racks = jnp.concatenate([racks_before, racks, racks_after], 0)
    rack_sum = jnp.dot(near_weights.astype(f32), near_racks, precision=HIGHEST) + rack_row[None, :]
    pod_sum = jnp.einsum(
        "tjs,jps->pt", all_weights.astype(f32).reshape(rows, slabs, rows), pods, precision=HIGHEST
    ).T

    host_drift = host_sum * (1.0 / (window * math.sqrt(day)))
    rack_drift = rack_sum * (1.0 / (window * math.sqrt(day * hosts_here / rack_count)))
    pod_drift = pod_sum * (1.0 / (window * math.sqrt(day * hosts_here / POD_DEV)))
    return host_drift, rack_drift, pod_drift


def solution(mesh):
    slabs, shards = (mesh.shape[name] for name in ("slab", "hst"))
    devices = mesh.devices.reshape(slabs // 2, 2, 2, shards // 8, 4)
    fine = Mesh(devices, ("y_hi", "core", "y_lo", "z", "x"))
    return jax.shard_map(
        on_device,
        mesh=fine,
        in_specs=(P(SLAB, HOST), P(HOST), P(HOST)),
        out_specs=(P(SLAB, HOST),) * 3,
        check_vma=False,
    )
```

time: 392 us -> 74.7 us (0.19)
  blocking collectives: 251 us -> 23.4 us
  starting transfers between devices: 63.7 us -> 27.2 us
  waiting for transfers between devices: 45.2 us -> 9.4 us
  between operations: 15.5 us -> 0.77 us
  matrix products: 8.4 us -> 12.5 us
    unnamed x1 -> x0, blocking collectives: 251 us -> none
    ppermute x5 -> x7, starting transfers between devices: 63.7 us -> 19.9 us  [the longest x6 18.1 us: ring(): lax.ppermute(value, axes, [(i, (i + steps) % count) for i in range(count)])]
    unnamed x2 -> x0, waiting for transfers between devices: 38.3 us -> none
    all_gather x0 -> x1, blocking collectives: none -> 23.4 us  [on_device(): lax.all_gather(sent, SLAB + ('y_lo',))]
    all_to_all x0 -> x1, waiting for transfers between devices: none -> 8.8 us  [on_device(): pod_part = lax.all_to_all(pod_part, ROW, 0, 0, tiled=True)]
    all_to_all x0 -> x1, starting transfers between devices: none -> 7.22 us  [on_device(): pod_part = lax.all_to_all(pod_part, ROW, 0, 0, tiled=True)]
    ppermute x5 -> x7, waiting for transfers between devices: 6.87 us -> 0.61 us  [the longest x6 0.6 us: ring(): lax.ppermute(value, axes, [(i, (i + steps) % count) for i in range(count)])]
    dot_general x6 -> x7, matrix products: 8.4 us -> 12.5 us  [the longest x1 4.12 us: on_device(): part = jnp.dot(load, member, preferred_element_type=f32)]
  transfers between devices with their start and end apart: 6 -> 8, of which waited for: 3 -> 2; matrix products, arithmetic and copies ran while one was open for 1% -> 13% of each run, Pallas kernels for 0% -> 0%
where the time goes in v1:
time: 74.7 us; the launch traced here: 74.4 us
  starting transfers between devices  27.2 us (36%)
  blocking collectives  23.4 us (31%)
  matrix products  12.5 us (17%)
  waiting for transfers between devices  9.4 us (13%)
  other arithmetic  0.97 us (1%)
  between operations  0.77 us (1%)
    all_gather x1, blocking collectives, on_device(): lax.all_gather(sent, SLAB + ('y_lo',))  23.4 us
    ppermute x6, starting transfers between devices, ring(): lax.ppermute(value, axes, [(i, (i + steps) % count) for i in range(count)])  18.1 us
    all_to_all x1, waiting for transfers between devices, on_device(): pod_part = lax.all_to_all(pod_part, ROW, 0, 0, tiled=True)  8.8 us
    all_to_all x1, starting transfers between devices, on_device(): pod_part = lax.all_to_all(pod_part, ROW, 0, 0, tiled=True)  7.22 us
    dot_general x1, matrix products, on_device(): part = jnp.dot(load, member, preferred_element_type=f32)  4.12 us
    dot_general x1, matrix products, on_device(): jnp.dot(near_weights.astype(bf16), near_load, preferred_element_type=f32)  3.68 us
    ppermute x1, starting transfers between devices, on_device(): lax.ppermute(far_row, SLAB, [(i, (i + slabs // 2) % slabs) for i in range...  1.85 us
    dot_general x1, matrix products, on_device(): jnp.dot(far_weights.astype(bf16), load, preferred_element_type=f32)  1.62 us
  transfers between devices with their start and end apart: 8, of which 2 were waited for; matrix products, arithmetic and copies ran while one was open for 13% of the time, Pallas kernels for 0%

profile of v1, /device:TPU:1, one launch (start us, length us, event | category | flops | bytes accessed | tf_op | source)
XLA Modules:
  0.0 74.4 jit_solution(15666470904172430360)
XLA Ops:
  0.6 4.4 %collective-permute-start = (bf16[72,8192]{1,0:T(8,128)(2,1)}, bf16[72,8192]{1,0:T(8,128)(2,1)S(1)}, u32[]{:S(2)}, u32[]{:S(2)}) collective-permute-start(bf16[72,8192]{1,0:T(8,128)(2,1)} %param.3), channel_id=1, source_target_pairs={{0,64},{64,128},{128,192},{192,0},{1,65},{65,129},{129,193},{193,1... | collective-permute-start | bytes 3538952 | tf_op jit(solution)/shard_map/ppermute | solution.py:18
  5.0 0.0 collective-permute-start.1
  5.0 1.6 %fusion.60 = f32[1,8192]{1,0:T(1,128)S(1)} fusion(bf16[72,8192]{1,0:T(8,128)(2,1)} %param.3, s32[]{:T(128)S(6)} %mul.66, s32[]{:T(128)S(6)} %mul.65), kind=kOutput, calls=%fused_computation.92 | convolution fusion | flops 1181664 | bytes 1212424 | tf_op jit(solution)/shard_map/dot_general | solution.py:53
  6.6 1.9 %collective-permute-start.2 = (f32[1,8192]{1,0:T(1,128)S(1)}, f32[1,8192]{1,0:T(1,128)S(1)}, u32[]{:S(2)}, u32[]{:S(2)}) collective-permute-start(f32[1,8192]{1,0:T(1,128)S(1)} %fusion.60), channel_id=1, source_target_pairs={{0,128},{64,192},{128,0},{192,64},{1,129},{65,193},{129,1},{193,65... | collective-permute-start | bytes 98312 | tf_op jit(solution)/shard_map/ppermute | solution.py:54
  8.5 0.8 %add_select_fusion = s32[8192]{0:T(1024)S(1)} fusion(s32[8192]{0:T(1024)} %param.4, s32[]{:T(128)S(6)} %mul.71), kind=kLoop, calls=%fused_computation.55 | loop fusion | flops 98304 | bytes 65540 | tf_op jit(solution)/shard_map/jit(remainder)/select_n | solution.py:56
  9.3 0.0 copy-start.1
  9.3 0.0 copy-start
  9.3 4.1 %fusion = f32[512,72]{0,1:T(8,128)S(1)} fusion(bf16[72,8192]{1,0:T(8,128)(2,1)} %param.3, s32[8192]{0:T(1024)S(1)} %add_select_fusion), kind=kOutput, calls=%fused_computation.1 | convolution fusion | flops 608174080 | bytes 1359872 | tf_op jit(solution)/shard_map/dot_general | solution.py:59
  13.4 0.1 collective-permute-start.3
  13.5 0.0 copy-done.1
  13.5 7.1 %collective-permute-start.6 = (s32[256]{0:T(256)S(1)}, s32[256]{0:T(256)S(1)}, u32[]{:S(2)}, u32[]{:S(2)}) collective-permute-start(s32[256]{0:T(256)S(1)} %copy-done.1), channel_id=1, source_target_pairs={{0,63},{1,0},{2,1},{3,2},{4,3},{5,4},{6,5},{7,6},{8,7},{9,8},{10,9... | collective-permute-start | bytes 3080 | tf_op jit(solution)/shard_map/ppermute | solution.py:18
  20.8 0.6 collective-permute-done.6
  21.4 0.9 %fusion.10 = f32[128,72]{1,0:T(8,128)} fusion(f32[512,72]{0,1:T(8,128)S(1)} %fusion, s32[512]{0:T(512)S(1)} %pad_add_fusion, s32[128]{0:T(128)S(1)} %fusion.54), kind=kOutput, calls=%fused_computation.14 | convolution fusion | flops 56688640 | bytes 186880 | tf_op jit(solution)/shard_map/dot_general | solution.py:68
  22.3 7.2 %all-to-all-start = ((f32[32,4,72]{2,1,0:T(4,128)}), f32[32,4,72]{2,1,0:T(4,128)S(1)}, u32[]{:S(2)}, u32[]{:S(2)}) async-start(f32[32,4,72]{2,1,0:T(4,128)} %bitcast.4), calls=%async_computation | async-start | bytes 131072 | tf_op jit(solution)/shard_map/all_to_all | solution.py:71
  29.6 8.8 %all-to-all-done = f32[32,4,72]{2,1,0:T(4,128)S(1)} async-done(((f32[32,4,72]{2,1,0:T(4,128)}), f32[32,4,72]{2,1,0:T(4,128)S(1)}, u32[]{:S(2)}, u32[]{:S(2)}) %all-to-all-start) | async-done | bytes 36896 | tf_op jit(solution)/shard_map/all_to_all | solution.py:71
  38.4 0.0 collective-permute-done.3
  38.4 6.4 %collective-permute-start.4 = (f32[72,256]{1,0:T(8,128)S(1)}, f32[72,256]{1,0:T(8,128)S(1)}, u32[]{:S(2)}, u32[]{:S(2)}) collective-permute-start(f32[72,256]{1,0:T(8,128)S(1)} %slice_add_fusion), channel_id=1, source_target_pairs={{0,64},{64,128},{128,192},{192,0},{1,65},{65,129},{129,193},{193,1... | collective-permute-start | bytes 221192 | tf_op jit(solution)/shard_map/ppermute | solution.py:18
  44.8 0.1 collective-permute-start.5
  44.9 0.1 fusion.58
  45.1 0.1 reshape.323
  45.2 23.4 %all-gather = f32[64,72]{1,0:T(8,128)S(1)} all-gather(f32[8,72]{1,0:T(8,128)S(1)} %pad_maximum_fusion), channel_id=2, replica_groups=mesh['y_hi'=2,'core'=2,'y_lo'=2,'z'=8,'x'=4] {'y_hi','core','y_lo'}, dimensions={0}, use_global_device_ids=true | all-gather | bytes 20736 | tf_op jit(solution)/shard_map/all_gather | solution.py:82
  68.6 1.0 %fusion.9 = f32[72,2]{0,1:T(2,128)} fusion(f32[4,2,72]{2,1,0:T(2,128)S(1)} %dynamic-slice_reduce_fusion, s32[4,72]{1,0:T(4,128)S(1)} %get-tuple-element.9, s32[4,72]{1,0:T(4,128)S(1)} %get-tuple-element.13, s32[4,72]{1,0:T(4,128)S(1)} %get-tuple-element.10, s32[4,72]{1,0:T(4,128)S(1)} %get-tuple-element.14, s32[4,72]{1,0:T(4,128)S(1)} %get-tuple-element.11, ...), kind=kOutput, calls=%fused_computation.13 | convolution fusion | flops 871056 | bytes 11232 | tf_op jit(solution)/shard_map/tjs,jps->pt/dot_general | solution.py:97
  69.6 0.1 reshape.325
  69.7 0.0 collective-permute-done.4
  69.7 0.0 collective-permute-done.5
  69.7 1.0 %fusion.8 = f32[72,256]{1,0:T(8,128)} fusion(f32[72,256]{1,0:T(8,128)S(1)} %collective-permute-done.5, f32[72,256]{1,0:T(8,128)S(1)} %slice_add_fusion, f32[72,256]{1,0:T(8,128)S(1)} %collective-permute-done.4, f32[256]{0:T(256)S(1)} %slice.16, s32[216]{0:T(256)S(1)} %get-tuple-element.4, s32[216]{0:T(256)S(1)} %get-tuple-element.7, ...), kind=kOutput, calls=%fused_computation.11 | convolution fusion | flops 48203136 | bytes 302272 | tf_op jit(solution)/shard_map/dot_general | solution.py:96
  70.7 0.0 collective-permute-done.2
  70.7 0.0 collective-permute-done
  70.7 0.0 collective-permute-done.1
  70.7 0.0 copy-done
  70.7 3.7 %fusion.1 = f32[72,8192]{1,0:T(8,128)} fusion(bf16[72,8192]{1,0:T(8,128)(2,1)} %collective-permute-done.1, bf16[72,8192]{1,0:T(8,128)(2,1)S(1)} %copy-done, bf16[72,8192]{1,0:T(8,128)(2,1)S(1)} %collective-permute-done, f32[8192]{0:T(1024)S(1)} %bitcast.26, s32[216]{0:T(256)S(1)} %get-tuple-element.4, s32[216]{0:T(256)S(1)} %get-tuple-element.7, ...), kind=kOutput, calls=%fused_computation.3 | convolution fusion | flops 266880384 | bytes 5937344 | tf_op jit(solution)/shard_map/dot_general | solution.py:94
  (20 shorter events, 0.2 us)
Async XLA Ops:
  0.6 70.1 %collective-permute-start = (bf16[72,8192]{1,0:T(8,128)(2,1)}, bf16[72,8192]{1,0:T(8,128)(2,1)S(1)}, u32[]{:S(2)}, u32[]{:S(2)}) collective-permute-start(bf16[72,8192]{1,0:T(8,128)(2,1)} %param.3), channel_id=1, source_target_pairs={{0,64},{64,128},{128,192},{192,0},{1,65},{65,129},{129,193},{193,1... | collective-permute-start | bytes 3538952 | tf_op jit(solution)/shard_map/ppermute | solution.py:18
  5.0 65.7 %collective-permute-start.1 = (bf16[72,8192]{1,0:T(8,128)(2,1)}, bf16[72,8192]{1,0:T(8,128)(2,1)}, u32[]{:S(2)}, u32[]{:S(2)}) collective-permute-start(bf16[72,8192]{1,0:T(8,128)(2,1)} %param.3), channel_id=1, source_target_pairs={{0,192},{64,0},{128,64},{192,128},{1,193},{65,1},{129,65},{193,129... | collective-permute-start | bytes 3538952 | tf_op jit(solution)/shard_map/ppermute | solution.py:18
  6.6 64.0 %collective-permute-start.2 = (f32[1,8192]{1,0:T(1,128)S(1)}, f32[1,8192]{1,0:T(1,128)S(1)}, u32[]{:S(2)}, u32[]{:S(2)}) collective-permute-start(f32[1,8192]{1,0:T(1,128)S(1)} %fusion.60), channel_id=1, source_target_pairs={{0,128},{64,192},{128,0},{192,64},{1,129},{65,193},{129,1},{193,65... | collective-permute-start | bytes 98312 | tf_op jit(solution)/shard_map/ppermute | solution.py:54
  9.3 4.3 %copy-start.1 = (s32[256]{0:T(256)S(1)}, s32[256]{0:T(256)}, u32[]{:S(2)}) copy-start(s32[256]{0:T(256)} %param.5) | copy-start | bytes 3076
  9.3 61.4 %copy-start = (bf16[72,8192]{1,0:T(8,128)(2,1)S(1)}, bf16[72,8192]{1,0:T(8,128)(2,1)}, u32[]{:S(2)}) copy-start(bf16[72,8192]{1,0:T(8,128)(2,1)} %param.3) | copy-start | bytes 3538948
  13.4 25.0 %collective-permute-start.3 = (f32[72,256]{1,0:T(8,128)S(1)}, f32[72,256]{1,0:T(8,128)S(1)}, u32[]{:S(2)}, u32[]{:S(2)}) collective-permute-start(f32[72,256]{1,0:T(8,128)S(1)} %slice.18), channel_id=1, source_target_pairs={{0,1},{1,2},{2,3},{3,4},{4,5},{5,6},{6,7},{7,8},{8,9},{9,10},{10,1... | collective-permute-start | bytes 221192 | tf_op jit(solution)/shard_map/ppermute | solution.py:18
  13.5 7.8 %collective-permute-start.6 = (s32[256]{0:T(256)S(1)}, s32[256]{0:T(256)S(1)}, u32[]{:S(2)}, u32[]{:S(2)}) collective-permute-start(s32[256]{0:T(256)S(1)} %copy-done.1), channel_id=1, source_target_pairs={{0,63},{1,0},{2,1},{3,2},{4,3},{5,4},{6,5},{7,6},{8,7},{9,8},{10,9... | collective-permute-start | bytes 3080 | tf_op jit(solution)/shard_map/ppermute | solution.py:18
  22.3 16.0 %all-to-all-start = ((f32[32,4,72]{2,1,0:T(4,128)}), f32[32,4,72]{2,1,0:T(4,128)S(1)}, u32[]{:S(2)}, u32[]{:S(2)}) async-start(f32[32,4,72]{2,1,0:T(4,128)} %bitcast.4), calls=%async_computation | async-start | bytes 131072 | tf_op jit(solution)/shard_map/all_to_all | solution.py:71
  38.4 31.3 %collective-permute-start.4 = (f32[72,256]{1,0:T(8,128)S(1)}, f32[72,256]{1,0:T(8,128)S(1)}, u32[]{:S(2)}, u32[]{:S(2)}) collective-permute-start(f32[72,256]{1,0:T(8,128)S(1)} %slice_add_fusion), channel_id=1, source_target_pairs={{0,64},{64,128},{128,192},{192,0},{1,65},{65,129},{129,193},{193,1... | collective-permute-start | bytes 221192 | tf_op jit(solution)/shard_map/ppermute | solution.py:18
  44.8 24.9 %collective-permute-start.5 = (f32[72,256]{1,0:T(8,128)S(1)}, f32[72,256]{1,0:T(8,128)S(1)}, u32[]{:S(2)}, u32[]{:S(2)}) collective-permute-start(f32[72,256]{1,0:T(8,128)S(1)} %slice_add_fusion), channel_id=1, source_target_pairs={{0,192},{64,0},{128,64},{192,128},{1,193},{65,1},{129,65},{193,129... | collective-permute-start | bytes 221192 | tf_op jit(solution)/shard_map/ppermute | solution.py:18

commit v2 on v1

v2 whole, which is shorter than its diff:
```python
import functools
import math

import jax
import jax.numpy as jnp
from jax import lax
from jax.experimental import pallas as pl
from jax.experimental.pallas import tpu as pltpu
from jax.sharding import Mesh, PartitionSpec as P

SLAB_LEN = 36
POD_DEV = 2
REACH = 2 * SLAB_LEN
WINDOW = 2 * REACH + 1
SLAB = ("y_hi", "core")
HOST = ("y_lo", "z", "x")
ROW = ("z", "x")
TILE = 8
HALF = 4
LANES = 128
BF16, F32, I32 = jnp.bfloat16, jnp.float32, jnp.int32
VMEM = pl.BlockSpec(memory_space=pltpu.VMEM)
SMEM = pl.BlockSpec(memory_space=pltpu.SMEM)
LIMIT = 62600000
NT = (((1,), (1,)), ((), ()))
NN = (((1,), (0,)), ((), ()))


def ring(value, axes, steps):
    count = lax.axis_size(axes)
    return lax.ppermute(value, axes, [(i, (i + steps) % count) for i in range(count)])


def overlap(last, low, high):
    return jnp.maximum(jnp.minimum(last, high) - jnp.maximum(low, 0) + 1, 0)


def weights(out_step, in_step, day):
    seen = jnp.zeros_like(out_step + in_step)
    for turn in (-day, 0, day):
        seen += overlap(out_step, in_step + turn - REACH, in_step + turn + REACH)
    return jnp.where(in_step <= out_step, WINDOW, 0) - seen


def thirds(value):
    high = value.astype(BF16)
    rest = value - high.astype(F32)
    middle = rest.astype(BF16)
    return high, middle, (rest - middle.astype(F32)).astype(BF16)


def exact_dot(small, value, dims):
    return sum(lax.dot_general(small, term, dims, preferred_element_type=F32) for term in thirds(value))


def rack_kernel(base_ref, slab_ref, load_ref, rack_ref, own_ref, next_ref, far_ref, *, racks, total, slabs):
    rows = load_ref.shape[0]
    slab = slab_ref[0]
    opposite = (slab + slabs // 2) % slabs

    @pl.when(pl.program_id(0) == 0)
    def _():
        own_ref[...] = jnp.zeros_like(own_ref)
        next_ref[...] = jnp.zeros_like(next_ref)

    local = rack_ref[...] - base_ref[0]
    local = jnp.where(local < 0, local + total, local)
    ahead = local >= racks
    local = jnp.where(ahead, local - racks, local)
    load = load_ref[...]
    ahead = jnp.broadcast_to(ahead.astype(F32), load.shape).astype(BF16)
    split = jnp.concatenate([load * (1 - ahead), load * ahead], 0)
    ids = lax.broadcasted_iota(I32, (racks, load.shape[1]), 0)
    member = (ids == local).astype(F32).astype(BF16)
    sums = lax.dot_general(split, member, NT, preferred_element_type=F32)
    own_ref[:rows] += sums[:rows]
    next_ref[:rows] += sums[rows:]
    day = rows * slabs
    step = lax.broadcasted_iota(I32, (rows, 1), 0)
    weight = weights(jnp.full_like(step, opposite * rows), slab * rows + step, day).astype(F32)
    far_ref[...] = jnp.sum(load.astype(F32) * weight, 0, keepdims=True)

    @pl.when(pl.program_id(0) == pl.num_programs(0) - 1)
    def _():
        for ref in (own_ref, next_ref):
            ref[rows : rows + 1] = jnp.sum(ref[:rows] * weight, 0, keepdims=True)


def total_kernel(own_ref, shifted_ref, far_ref, pod_ref, out_ref, rack_ref, sent_ref, *, per_row):
    rows, racks = rack_ref.shape
    total = own_ref[:rows] + shifted_ref[:rows]
    rack_ref[...] = total
    pod = pod_ref[...]
    shard = pod // POD_DEV
    place = shard % per_row * HALF + shard // per_row * POD_DEV + pod % POD_DEV
    count = out_ref.shape[0] * HALF
    member = (lax.broadcasted_iota(I32, (count, racks), 0) == place).astype(F32).astype(BF16)
    pods = exact_dot(member, total, NT)
    pods = jnp.concatenate([pods, jnp.zeros((count, out_ref.shape[2] - rows), F32)], 1)
    for i in range(out_ref.shape[0]):
        out_ref[i] = pods[HALF * i : HALF * (i + 1)]
    hosts = far_ref.shape[1]
    sent_ref[:, :hosts] = far_ref[...]
    sent_ref[:, hosts:] = own_ref[rows : rows + 1] + shifted_ref[rows : rows + 1]


def pack_kernel(got_ref, out_ref, *, slabs, lines):
    pods = jnp.sum(got_ref[...], 0)
    for line in range(lines):
        tile = jnp.concatenate([pods[line * POD_DEV : (line + 1) * POD_DEV], jnp.zeros((TILE - POD_DEV, LANES), F32)], 0)
        for slab in range(slabs):
            out_ref[slab * lines + line] = tile


def group_kernel(slab_ref, got_ref, cross_ref, own_ref, core_ref, far_ref, rack_ref, pod_ref, *, slabs, lines, rack_scale, pod_scale):
    rows, racks = own_ref.shape
    day = rows * slabs
    slab = slab_ref[0]
    out_step = slab * rows + lax.broadcasted_iota(I32, (rows, rows), 0)
    step = lax.broadcasted_iota(I32, (rows, rows), 1)
    core_slab = slab + 1 - 2 * (slab % 2)
    cross_slab = (slab + 2 * (slab % 2) - 1 + slabs) % slabs
    total = 0
    for other, ref in ((cross_slab, cross_ref), (slab, own_ref), (core_slab, core_ref)):
        total += exact_dot(weights(out_step, other * rows + step, day).astype(F32).astype(BF16), ref[...], NN)
    rack_ref[...] = (total + far_ref[:, far_ref.shape[1] - racks :]) * rack_scale
    pods = 0
    for other in range(slabs):
        part = sum(got_ref[other * lines + line] for line in range(lines))[:, :rows]
        matrix = weights(out_step, other * rows + step, day).astype(F32).astype(BF16)
        pods += sum(lax.dot_general(term, matrix, NT, preferred_element_type=F32) for term in thirds(part))
    pod_ref[...] = pods[:POD_DEV] * pod_scale


def call(kernel, ins, outs, name, limit=16 << 20, **more):
    return pl.pallas_call(
        kernel,
        in_specs=ins,
        out_shape=[jax.ShapeDtypeStruct(shape, F32) for shape in outs],
        compiler_params=pltpu.CompilerParams(vmem_limit_bytes=limit),
        cost_estimate=pl.CostEstimate(flops=1, bytes_accessed=1, transcendentals=0),
        name=name,
        **more,
    )


def on_device(load, host_rack, rack_pod):
    rows, hosts = load.shape
    racks = rack_pod.shape[0]
    slabs = lax.axis_size(SLAB)
    shards = lax.axis_size(HOST)
    row_size = lax.axis_size(ROW)
    lines = lax.axis_size("y_lo")
    day = rows * slabs
    slab = lax.axis_index(SLAB)
    base = lax.axis_index(HOST) * racks

    across = [(i, (i + 2 * (i % 2) - 1) % slabs) for i in range(slabs)]
    mates = [(0, 1), (1, 0)]
    cross = lax.ppermute(load, SLAB, across)

    block = 2048
    tall = rows + TILE
    own_part, next_part, far_part = call(
        functools.partial(rack_kernel, racks=racks, total=racks * shards, slabs=slabs),
        [SMEM, SMEM, pl.BlockSpec((rows, block), lambda i: (0, i)), pl.BlockSpec((1, block), lambda i: (0, i))],
        [(tall, racks), (tall, racks), (1, hosts)],
        "rack_sums",
        LIMIT,
        grid=(hosts // block,),
        out_specs=[pl.BlockSpec((tall, racks), lambda i: (0, 0))] * 2 + [pl.BlockSpec((1, block), lambda i: (0, i))],
    )(base.reshape(1), slab.reshape(1), load, host_rack.reshape(1, hosts))
    shifted = ring(next_part, HOST, 1)
    pod_part, rack_own, far_sent = call(
        functools.partial(total_kernel, per_row=row_size),
        [VMEM] * 4,
        [(row_size, HALF, LANES), (rows, racks), (1, hosts + racks)],
        "totals",
        out_specs=[VMEM] * 3,
    )(own_part, shifted, far_part, rack_pod.reshape(1, racks))

    later, pod_part, rack_own, far_sent = lax.optimization_barrier((load, pod_part, rack_own, far_sent))
    got = lax.all_to_all(pod_part, ROW, 0, 0, tiled=True)
    core = lax.ppermute(later, "core", mates)
    rack_core = lax.ppermute(rack_own, "core", mates)
    rack_cross = lax.ppermute(rack_own, SLAB, across)
    far = lax.ppermute(far_sent, SLAB, [(0, 2), (3, 1)])

    (sent,) = call(
        functools.partial(pack_kernel, slabs=slabs, lines=lines),
        [VMEM],
        [(slabs * lines, TILE, LANES)],
        "pack",
        out_specs=[VMEM],
    )(got)
    far, _ = lax.optimization_barrier((far, sent))
    got = lax.all_to_all(sent, SLAB + ("y_lo",), 0, 0, tiled=True)

    out_step = slab * rows + lax.broadcasted_iota(I32, (rows, 1), 0)
    near = lax.broadcasted_iota(I32, (1, 3 * rows), 1)
    turn = 1 - 2 * (slab % 2)
    origin = jnp.where(near < rows, slab - turn, jnp.where(near < 2 * rows, slab, slab + turn))
    near_step = (origin + slabs) % slabs * rows + near % rows
    near_weights = weights(out_step, near_step, day)
    near_load = jnp.concatenate([cross, later, core], 0)
    host_sum = jnp.dot(near_weights.astype(BF16), near_load, preferred_element_type=F32) + far[:, :hosts]
    host_drift = host_sum * (1.0 / (WINDOW * math.sqrt(day)))

    got, host_drift = lax.optimization_barrier((got, host_drift))
    rack_drift, pod_drift = call(
        functools.partial(
            group_kernel,
            slabs=slabs,
            lines=lines,
            rack_scale=1.0 / (WINDOW * math.sqrt(day * hosts / racks)),
            pod_scale=1.0 / (WINDOW * math.sqrt(day * hosts / POD_DEV)),
        ),
        [SMEM] + [VMEM] * 5,
        [(rows, racks), (POD_DEV, rows)],
        "groups",
        out_specs=[VMEM] * 2,
    )(slab.reshape(1), got, rack_cross, rack_own, rack_core, far)
    return host_drift, rack_drift, pod_drift.T


def solution(mesh):
    slabs, shards = (mesh.shape[name] for name in ("slab", "hst"))
    devices = mesh.devices.reshape(slabs // 2, 2, 2, shards // 8, 4)
    fine = Mesh(devices, ("y_hi", "core", "y_lo", "z", "x"))
    return jax.shard_map(
        on_device,
        mesh=fine,
        in_specs=(P(SLAB, HOST), P(HOST), P(HOST)),
        out_specs=(P(SLAB, HOST),) * 3,
        check_vma=False,
    )
```

time: 74.7 us -> 47.9 us (0.64)
  blocking collectives: 23.4 us -> 0 us
  matrix products: 12.5 us -> 3.78 us
  Pallas kernels: 0 us -> 6.99 us
  starting transfers between devices: 27.2 us -> 23.2 us
  local copies, waits for them, and re-layouts: 0.21 us -> 2.33 us
  waiting for transfers between devices: 9.4 us -> 10.4 us
  other arithmetic: 0.97 us -> 0.02 us
    all_gather x1 -> x0, blocking collectives: 23.4 us -> none  [on_device(): lax.all_gather(sent, SLAB + ('y_lo',))]
    ppermute x6 -> x1, starting transfers between devices: 18.1 us -> 2.04 us  [ring(): lax.ppermute(value, axes, [(i, (i + steps) % count) for i in range(count)])]
    ppermute x1 -> x5, starting transfers between devices: 1.85 us -> 10.7 us  [the longest x1 3.76 us: on_device(): cross = lax.ppermute(load, SLAB, across)]
    dot_general x7 -> x1, matrix products: 12.5 us -> 3.78 us  [on_device(): jnp.dot(near_weights.astype(BF16), near_load, preferred_element_type=F32)]
    pallas_call x0 -> x4, Pallas kernels: none -> 6.99 us  [the longest x1 4.44 us: on_device(): call(functools.partial(rack_kernel, racks=racks, total=racks * shards, sl...]
    ppermute x6 -> x1, waiting for transfers between devices: 0.6 us -> 6.18 us  [ring(): lax.ppermute(value, axes, [(i, (i + steps) % count) for i in range(count)])]
    all_to_all x1 -> x2, waiting for transfers between devices: 8.8 us -> 4.2 us  [the longest x1 3.33 us: on_device(): got = lax.all_to_all(pod_part, ROW, 0, 0, tiled=True)]
    all_to_all x1 -> x2, starting transfers between devices: 7.22 us -> 10.5 us  [the longest x1 5.78 us: on_device(): got = lax.all_to_all(sent, SLAB + ('y_lo',), 0, 0, tiled=True)]
  transfers between devices with their start and end apart: 8 -> 8, of which waited for: 2 -> 3; matrix products, arithmetic and copies ran while one was open for 13% -> 8% of each run, Pallas kernels for 0% -> 3%
where the time goes in v2:
time: 47.9 us; the launch traced here: 47.4 us
  starting transfers between devices  23.2 us (48%)
  waiting for transfers between devices  10.4 us (22%)
  Pallas kernels  6.99 us (15%)
  matrix products  3.78 us (8%)
  local copies, waits for them, and re-layouts  2.33 us (5%)
  between operations  0.71 us (1%)
    ppermute x1, waiting for transfers between devices, ring(): lax.ppermute(value, axes, [(i, (i + steps) % count) for i in range(count)])  6.18 us
    all_to_all x1, starting transfers between devices, on_device(): got = lax.all_to_all(sent, SLAB + ('y_lo',), 0, 0, tiled=True)  5.78 us
    all_to_all x1, starting transfers between devices, on_device(): got = lax.all_to_all(pod_part, ROW, 0, 0, tiled=True)  4.75 us
    pallas_call x1, Pallas kernels, on_device(): call(functools.partial(rack_kernel, racks=racks, total=racks * shards, sl...  4.44 us
    dot_general x1, matrix products, on_device(): jnp.dot(near_weights.astype(BF16), near_load, preferred_element_type=F32)  3.78 us
    ppermute x1, starting transfers between devices, on_device(): cross = lax.ppermute(load, SLAB, across)  3.76 us
    all_to_all x1, waiting for transfers between devices, on_device(): got = lax.all_to_all(pod_part, ROW, 0, 0, tiled=True)  3.33 us
    ppermute x1, starting transfers between devices, on_device(): rack_cross = lax.ppermute(rack_own, SLAB, across)  3.17 us
  transfers between devices with their start and end apart: 8, of which 3 were waited for; matrix products, arithmetic and copies ran while one was open for 8% of the time, Pallas kernels for 3%

profile of v2, /device:TPU:1, one launch (start us, length us, event | category | flops | bytes accessed | tf_op | source)
XLA Modules:
  0.0 47.4 jit_solution(16337137488843714509)
XLA Ops:
  0.6 4.4 %rack_sums.1 = (f32[80,256]{1,0:T(8,128)}, f32[80,256]{1,0:T(8,128)}, f32[1,8192]{1,0:T(1,128)}) custom-call(s32[1]{0:T(128)} %bitcast.base_ref, s32[1]{0:T(128)} %bitcast.1.slab_ref, bf16[72,8192]{1,0:T(8,128)(2,1)} %load_ref.1, s32[1,8192]{1,0:T(1,128)} %bitcast.7), custom_call_target="tpu_custom_call" | custom-call | flops 1 | bytes 1 | tf_op jit(solution)/shard_map/rack_sums/pallas_call | solution.py:164
  5.1 2.0 %collective-permute-start = (f32[80,256]{1,0:T(8,128)}, f32[80,256]{1,0:T(8,128)S(1)}, u32[]{:S(2)}, u32[]{:S(2)}) collective-permute-start(f32[80,256]{1,0:T(8,128)} %get-tuple-element.19), channel_id=1, source_target_pairs={{0,1},{1,2},{2,3},{3,4},{4,5},{5,6},{6,7},{7,8},{8,9},{9,10},{10,1... | collective-permute-start | bytes 245768 | tf_op jit(solution)/shard_map/ppermute | solution.py:31
  7.1 3.8 %collective-permute-start.1 = (bf16[72,8192]{1,0:T(8,128)(2,1)}, bf16[72,8192]{1,0:T(8,128)(2,1)S(1)}, u32[]{:S(2)}, u32[]{:S(2)}) collective-permute-start(bf16[72,8192]{1,0:T(8,128)(2,1)} %load_ref.1), channel_id=1, source_target_pairs={{0,192},{64,128},{128,64},{192,0},{1,193},{65,129},{129,65},{193,1... | collective-permute-start | bytes 3538952 | tf_op jit(solution)/shard_map/ppermute | solution.py:160
  10.9 6.2 %collective-permute-done.shifted_ref = f32[80,256]{1,0:T(8,128)S(1)} collective-permute-done((f32[80,256]{1,0:T(8,128)}, f32[80,256]{1,0:T(8,128)S(1)}, u32[]{:S(2)}, u32[]{:S(2)}) %collective-permute-start) | collective-permute-done | bytes 81952 | tf_op jit(solution)/shard_map/ppermute | solution.py:31
  17.1 0.0 copy-start
  17.1 0.9 %copy-done = f32[80,256]{1,0:T(8,128)S(1)} copy-done((f32[80,256]{1,0:T(8,128)S(1)}, f32[80,256]{1,0:T(8,128)}, u32[]{:S(2)}) %copy-start) | copy-done | bytes 81944
  17.9 0.0 copy-start.1
  17.9 0.8 %copy-done.1 = f32[1,8192]{1,0:T(1,128)S(1)} copy-done((f32[1,8192]{1,0:T(1,128)S(1)}, f32[1,8192]{1,0:T(1,128)}, u32[]{:S(2)}) %copy-start.1) | copy-done | bytes 32792
  18.7 0.0 copy-start.2
  18.7 0.7 %copy-done.2 = s32[256]{0:T(256)S(1)} copy-done((s32[256]{0:T(256)S(1)}, s32[256]{0:T(256)}, u32[]{:S(2)}) %copy-start.2) | copy-done | bytes 1048
  19.4 0.8 %totals.1 = (f32[32,4,128]{2,1,0:T(4,128)}, f32[72,256]{1,0:T(8,128)S(1)}, f32[1,8448]{1,0:T(1,128)S(1)}) custom-call(f32[80,256]{1,0:T(8,128)S(1)} %copy-done, f32[80,256]{1,0:T(8,128)S(1)} %collective-permute-done.shifted_ref, f32[1,8192]{1,0:T(1,128)S(1)} %copy-done.1, s32[1,256]{1,0:T(1,128)S(1)} %bitcast.6), custom_call_target="tpu_custom_call" | custom-call | flops 1 | bytes 1 | tf_op jit(solution)/shard_map/totals/pallas_call | solution.py:174
  20.2 1.3 %collective-permute-start.2 = (bf16[72,8192]{1,0:T(8,128)(2,1)}, bf16[72,8192]{1,0:T(8,128)(2,1)S(1)}, u32[]{:S(2)}, u32[]{:S(2)}) collective-permute-start(bf16[72,8192]{1,0:T(8,128)(2,1)} %load_ref.1), channel_id=1, source_target_pairs={{0,64},{64,0},{1,65},{65,1},{2,66},{66,2},{3,67},{67,3},{4,68},{68... | collective-permute-start | bytes 3538952 | tf_op jit(solution)/shard_map/ppermute | solution.py:184
  21.6 4.7 %all-to-all-start = ((f32[32,4,128]{2,1,0:T(4,128)}), f32[32,4,128]{2,1,0:T(4,128)S(1)}, u32[]{:S(2)}, u32[]{:S(2)}) async-start(f32[32,4,128]{2,1,0:T(4,128)} %get-tuple-element.24), calls=%async_computation | async-start | bytes 131072 | tf_op jit(solution)/shard_map/all_to_all | solution.py:183
  26.3 1.3 %collective-permute-start.3 = (f32[1,8448]{1,0:T(1,128)S(1)}, f32[1,8448]{1,0:T(1,128)S(1)}, u32[]{:S(2)}, u32[]{:S(2)}) collective-permute-start(f32[1,8448]{1,0:T(1,128)S(1)} %get-tuple-element.26), channel_id=1, source_target_pairs={{0,128},{192,64},{1,129},{193,65},{2,130},{194,66},{3,131},{195,67... | collective-permute-start | bytes 101384 | tf_op jit(solution)/shard_map/ppermute | solution.py:187
  27.7 3.2 %collective-permute-start.4 = (f32[72,256]{1,0:T(8,128)S(1)}, f32[72,256]{1,0:T(8,128)S(1)}, u32[]{:S(2)}, u32[]{:S(2)}) collective-permute-start(f32[72,256]{1,0:T(8,128)S(1)} %get-tuple-element.30.own_ref), channel_id=1, source_target_pairs={{0,192},{64,128},{128,64},{192,0},{1,193},{65,129},{129,65},{193,1... | collective-permute-start | bytes 221192 | tf_op jit(solution)/shard_map/ppermute | solution.py:186
  30.8 1.1 %collective-permute-start.5 = (f32[72,256]{1,0:T(8,128)S(1)}, f32[72,256]{1,0:T(8,128)S(1)}, u32[]{:S(2)}, u32[]{:S(2)}) collective-permute-start(f32[72,256]{1,0:T(8,128)S(1)} %get-tuple-element.30.own_ref), channel_id=1, source_target_pairs={{0,64},{64,0},{1,65},{65,1},{2,66},{66,2},{3,67},{67,3},{4,68},{68... | collective-permute-start | bytes 221192 | tf_op jit(solution)/shard_map/ppermute | solution.py:185
  31.9 3.3 %all-to-all-done.got_ref = f32[32,4,128]{2,1,0:T(4,128)S(1)} async-done(((f32[32,4,128]{2,1,0:T(4,128)}), f32[32,4,128]{2,1,0:T(4,128)S(1)}, u32[]{:S(2)}, u32[]{:S(2)}) %all-to-all-start) | async-done | bytes 65568 | tf_op jit(solution)/shard_map/all_to_all | solution.py:183
  35.3 0.7 %pack.1 = f32[8,8,128]{2,1,0:T(8,128)} custom-call(f32[32,4,128]{2,1,0:T(4,128)S(1)} %all-to-all-done.got_ref), custom_call_target="tpu_custom_call" | custom-call | flops 1 | bytes 1 | tf_op jit(solution)/shard_map/pack/pallas_call | solution.py:189
  35.9 5.8 %all-to-all-start.1 = ((f32[8,8,128]{2,1,0:T(8,128)}), f32[8,8,128]{2,1,0:T(8,128)S(1)}, u32[]{:S(2)}, u32[]{:S(2)}) async-start(f32[8,8,128]{2,1,0:T(8,128)} %pack.1), calls=%async_computation.1 | async-start | bytes 65536 | tf_op jit(solution)/shard_map/all_to_all | solution.py:197
  41.7 0.0 collective-permute-done.3.far_ref
  41.7 0.0 collective-permute-done.1
  41.7 0.0 collective-permute-done.2
  41.7 3.8 %fusion = f32[72,8192]{1,0:T(8,128)} fusion(bf16[72,8192]{1,0:T(8,128)(2,1)S(1)} %collective-permute-done.2, bf16[72,8192]{1,0:T(8,128)(2,1)} %load_ref.1, bf16[72,8192]{1,0:T(8,128)(2,1)S(1)} %collective-permute-done.1, f32[8192]{0:T(1024)S(1)} %bitcast.8, s32[216]{0:T(256)S(1)} %get-tuple-element.39, s32[216]{0:T(256)S(1)} %get-tuple-element.36, ...), kind=kOutput, calls=%fused_computation.1 | convolution fusion | flops 266880384 | bytes 5937344 | tf_op jit(solution)/shard_map/dot_general | solution.py:206
  45.5 0.9 %all-to-all-done.1.got_ref = f32[8,8,128]{2,1,0:T(8,128)S(1)} async-done(((f32[8,8,128]{2,1,0:T(8,128)}), f32[8,8,128]{2,1,0:T(8,128)S(1)}, u32[]{:S(2)}, u32[]{:S(2)}) %all-to-all-start.1) | async-done | bytes 32800 | tf_op jit(solution)/shard_map/all_to_all | solution.py:197
  46.4 0.0 collective-permute-done.4.cross_ref
  46.4 0.0 collective-permute-done.5.core_ref
  46.4 1.1 %groups.1 = (f32[72,256]{1,0:T(8,128)}, f32[2,72]{1,0:T(2,128)}) custom-call(s32[1]{0:T(128)} %bitcast.1.slab_ref, f32[8,8,128]{2,1,0:T(8,128)S(1)} %all-to-all-done.1.got_ref, f32[72,256]{1,0:T(8,128)S(1)} %collective-permute-done.4.cross_ref, f32[72,256]{1,0:T(8,128)S(1)} %get-tuple-element.30.own_ref, f32[72,256]{1,0:T(8,128)S(1)} %collective-permute-done.5.core_ref, ...), custom_call_target="tpu_custom_call" | custom-call | flops 1 | bytes 1 | tf_op jit(solution)/shard_map/groups/pallas_call | solution.py:210
  (4 shorter events, 0.0 us)
Async XLA Ops:
  5.1 12.0 %collective-permute-start = (f32[80,256]{1,0:T(8,128)}, f32[80,256]{1,0:T(8,128)S(1)}, u32[]{:S(2)}, u32[]{:S(2)}) collective-permute-start(f32[80,256]{1,0:T(8,128)} %get-tuple-element.19), channel_id=1, source_target_pairs={{0,1},{1,2},{2,3},{3,4},{4,5},{5,6},{6,7},{7,8},{8,9},{9,10},{10,1... | collective-permute-start | bytes 245768 | tf_op jit(solution)/shard_map/ppermute | solution.py:31
  7.1 34.6 %collective-permute-start.1 = (bf16[72,8192]{1,0:T(8,128)(2,1)}, bf16[72,8192]{1,0:T(8,128)(2,1)S(1)}, u32[]{:S(2)}, u32[]{:S(2)}) collective-permute-start(bf16[72,8192]{1,0:T(8,128)(2,1)} %load_ref.1), channel_id=1, source_target_pairs={{0,192},{64,128},{128,64},{192,0},{1,193},{65,129},{129,65},{193,1... | collective-permute-start | bytes 3538952 | tf_op jit(solution)/shard_map/ppermute | solution.py:160
  17.1 0.9 %copy-start = (f32[80,256]{1,0:T(8,128)S(1)}, f32[80,256]{1,0:T(8,128)}, u32[]{:S(2)}) copy-start(f32[80,256]{1,0:T(8,128)} %get-tuple-element.18.own_ref) | copy-start | bytes 245764
  17.9 0.8 %copy-start.1 = (f32[1,8192]{1,0:T(1,128)S(1)}, f32[1,8192]{1,0:T(1,128)}, u32[]{:S(2)}) copy-start(f32[1,8192]{1,0:T(1,128)} %get-tuple-element.20.far_ref) | copy-start | bytes 98308
  18.7 0.7 %copy-start.2 = (s32[256]{0:T(256)S(1)}, s32[256]{0:T(256)}, u32[]{:S(2)}) copy-start(s32[256]{0:T(256)} %param.5) | copy-start | bytes 3076
  20.2 21.5 %collective-permute-start.2 = (bf16[72,8192]{1,0:T(8,128)(2,1)}, bf16[72,8192]{1,0:T(8,128)(2,1)S(1)}, u32[]{:S(2)}, u32[]{:S(2)}) collective-permute-start(bf16[72,8192]{1,0:T(8,128)(2,1)} %load_ref.1), channel_id=1, source_target_pairs={{0,64},{64,0},{1,65},{65,1},{2,66},{66,2},{3,67},{67,3},{4,68},{68... | collective-permute-start | bytes 3538952 | tf_op jit(solution)/shard_map/ppermute | solution.py:184
  21.6 13.7 %all-to-all-start = ((f32[32,4,128]{2,1,0:T(4,128)}), f32[32,4,128]{2,1,0:T(4,128)S(1)}, u32[]{:S(2)}, u32[]{:S(2)}) async-start(f32[32,4,128]{2,1,0:T(4,128)} %get-tuple-element.24), calls=%async_computation | async-start | bytes 131072 | tf_op jit(solution)/shard_map/all_to_all | solution.py:183
  26.3 15.4 %collective-permute-start.3 = (f32[1,8448]{1,0:T(1,128)S(1)}, f32[1,8448]{1,0:T(1,128)S(1)}, u32[]{:S(2)}, u32[]{:S(2)}) collective-permute-start(f32[1,8448]{1,0:T(1,128)S(1)} %get-tuple-element.26), channel_id=1, source_target_pairs={{0,128},{192,64},{1,129},{193,65},{2,130},{194,66},{3,131},{195,67... | collective-permute-start | bytes 101384 | tf_op jit(solution)/shard_map/ppermute | solution.py:187
  27.7 18.7 %collective-permute-start.4 = (f32[72,256]{1,0:T(8,128)S(1)}, f32[72,256]{1,0:T(8,128)S(1)}, u32[]{:S(2)}, u32[]{:S(2)}) collective-permute-start(f32[72,256]{1,0:T(8,128)S(1)} %get-tuple-element.30.own_ref), channel_id=1, source_target_pairs={{0,192},{64,128},{128,64},{192,0},{1,193},{65,129},{129,65},{193,1... | collective-permute-start | bytes 221192 | tf_op jit(solution)/shard_map/ppermute | solution.py:186
  30.8 15.6 %collective-permute-start.5 = (f32[72,256]{1,0:T(8,128)S(1)}, f32[72,256]{1,0:T(8,128)S(1)}, u32[]{:S(2)}, u32[]{:S(2)}) collective-permute-start(f32[72,256]{1,0:T(8,128)S(1)} %get-tuple-element.30.own_ref), channel_id=1, source_target_pairs={{0,64},{64,0},{1,65},{65,1},{2,66},{66,2},{3,67},{67,3},{4,68},{68... | collective-permute-start | bytes 221192 | tf_op jit(solution)/shard_map/ppermute | solution.py:185
  35.9 10.5 %all-to-all-start.1 = ((f32[8,8,128]{2,1,0:T(8,128)}), f32[8,8,128]{2,1,0:T(8,128)S(1)}, u32[]{:S(2)}, u32[]{:S(2)}) async-start(f32[8,8,128]{2,1,0:T(8,128)} %pack.1), calls=%async_computation.1 | async-start | bytes 65536 | tf_op jit(solution)/shard_map/all_to_all | solution.py:197

commit v3 on v2

--- a/solution.py
+++ b/solution.py
@@ -20,6 +20,7 @@
 LANES = 128
 BF16, F32, I32 = jnp.bfloat16, jnp.float32, jnp.int32
 VMEM = pl.BlockSpec(memory_space=pltpu.VMEM)
+HBM = pl.BlockSpec(memory_space=pltpu.HBM)
 SMEM = pl.BlockSpec(memory_space=pltpu.SMEM)
 LIMIT = 62600000
 NT = (((1,), (1,)), ((), ()))
@@ -112,6 +113,35 @@
             out_ref[slab * lines + line] = tile
 
 
+def host_kernel(slab_ref, cross_ref, load_hbm, core_ref, far_ref, out_hbm, load_ref, out_ref, in_sems, sems, *, slabs, blocks, scale):
+    rows, hosts = load_ref.shape
+    width = hosts // blocks
+    arrivals = []
+    for i in range(blocks):
+        part = pl.ds(i * width, width)
+        arrivals.append(pltpu.make_async_copy(load_hbm.at[:, part], load_ref.at[:, part], in_sems.at[i]))
+        arrivals[-1].start()
+    day = rows * slabs
+    slab = slab_ref[0]
+    turn = 1 - 2 * (slab % 2)
+    out_step = slab * rows + lax.broadcasted_iota(I32, (rows, rows), 0)
+    step = lax.broadcasted_iota(I32, (rows, rows), 1)
+    parts = [weights(out_step, (other + slabs) % slabs * rows + step, day) for other in (slab - turn, slab, slab + turn)]
+    matrix = jnp.concatenate([part.astype(F32) for part in parts], 1).astype(BF16)
+    copies = []
+    for i in range(blocks):
+        part = slice(i * width, (i + 1) * width)
+        arrivals[i].wait()
+        near = jnp.concatenate([ref[:, part] for ref in (cross_ref, load_ref, core_ref)], 0)
+        sums = lax.dot_general(matrix, near, NN, preferred_element_type=F32)
+        out_ref[:, part] = (sums + far_ref[:, part]) * scale
+        part = pl.ds(i * width, width)
+        copies.append(pltpu.make_async_copy(out_ref.at[:, part], out_hbm.at[:, part], sems.at[i]))
+        copies[-1].start()
+    for copy in copies:
+        copy.wait()
+
+
 def group_kernel(slab_ref, got_ref, cross_ref, own_ref, core_ref, far_ref, rack_ref, pod_ref, *, slabs, lines, rack_scale, pod_scale):
     rows, racks = own_ref.shape
     day = rows * slabs
@@ -132,7 +162,7 @@
     pod_ref[...] = pods[:POD_DEV] * pod_scale
 
 
-def call(kernel, ins, outs, name, limit=16 << 20, **more):
+def call(kernel, ins, outs, name, limit=6 << 20, **more):
     return pl.pallas_call(
         kernel,
         in_specs=ins,
@@ -158,19 +188,22 @@
     across = [(i, (i + 2 * (i % 2) - 1) % slabs) for i in range(slabs)]
     mates = [(0, 1), (1, 0)]
     cross = lax.ppermute(load, SLAB, across)
-
-    block = 2048
+    core = lax.ppermute(load, "core", mates)
+
+    blocks = 8
+    block = 4096
     tall = rows + TILE
     own_part, next_part, far_part = call(
         functools.partial(rack_kernel, racks=racks, total=racks * shards, slabs=slabs),
         [SMEM, SMEM, pl.BlockSpec((rows, block), lambda i: (0, i)), pl.BlockSpec((1, block), lambda i: (0, i))],
         [(tall, racks), (tall, racks), (1, hosts)],
         "rack_sums",
-        LIMIT,
+        12 << 20,
         grid=(hosts // block,),
         out_specs=[pl.BlockSpec((tall, racks), lambda i: (0, 0))] * 2 + [pl.BlockSpec((1, block), lambda i: (0, i))],
-    )(base.reshape(1), slab.reshape(1), load, host_rack.reshape(1, hosts))
+    )(base.reshape(1), slab.reshape(1), *(pltpu.with_memory_space_constraint(x, pltpu.HBM) for x in (load, host_rack.reshape(1, hosts))))
     shifted = ring(next_part, HOST, 1)
+    far_part, core = lax.optimization_barrier((far_part, core))
     pod_part, rack_own, far_sent = call(
         functools.partial(total_kernel, per_row=row_size),
         [VMEM] * 4,
@@ -181,7 +214,6 @@
 
     later, pod_part, rack_own, far_sent = lax.optimization_barrier((load, pod_part, rack_own, far_sent))
     got = lax.all_to_all(pod_part, ROW, 0, 0, tiled=True)
-    core = lax.ppermute(later, "core", mates)
     rack_core = lax.ppermute(rack_own, "core", mates)
     rack_cross = lax.ppermute(rack_own, SLAB, across)
     far = lax.ppermute(far_sent, SLAB, [(0, 2), (3, 1)])
@@ -196,16 +228,19 @@
     far, _ = lax.optimization_barrier((far, sent))
     got = lax.all_to_all(sent, SLAB + ("y_lo",), 0, 0, tiled=True)
 
-    out_step = slab * rows + lax.broadcasted_iota(I32, (rows, 1), 0)
-    near = lax.broadcasted_iota(I32, (1, 3 * rows), 1)
-    turn = 1 - 2 * (slab % 2)
-    origin = jnp.where(near < rows, slab - turn, jnp.where(near < 2 * rows, slab, slab + turn))
-    near_step = (origin + slabs) % slabs * rows + near % rows
-    near_weights = weights(out_step, near_step, day)
-    near_load = jnp.concatenate([cross, later, core], 0)
-    host_sum = jnp.dot(near_weights.astype(BF16), near_load, preferred_element_type=F32) + far[:, :hosts]
-    host_drift = host_sum * (1.0 / (WINDOW * math.sqrt(day)))
-
+    (host_drift,) = call(
+        functools.partial(host_kernel, slabs=slabs, blocks=blocks, scale=1.0 / (WINDOW * math.sqrt(day))),
+        [SMEM, VMEM, HBM, VMEM, VMEM],
+        [(rows, hosts)],
+        "host_sums",
+        out_specs=[HBM],
+        scratch_shapes=[
+            pltpu.VMEM((rows, hosts), BF16),
+            pltpu.VMEM((rows, hosts), F32),
+            pltpu.SemaphoreType.DMA((blocks,)),
+            pltpu.SemaphoreType.DMA((blocks,)),
+        ],
+    )(slab.reshape(1), cross, pltpu.with_memory_space_constraint(load, pltpu.HBM), core, far)
     got, host_drift = lax.optimization_barrier((got, host_drift))
     rack_drift, pod_drift = call(
         functools.partial(

time: 47.9 us -> 46 us (0.960)
  waiting for transfers between devices: 10.4 us -> 15.9 us
  matrix products: 3.78 us -> 0 us
  starting transfers between devices: 23.2 us -> 20.2 us
  local copies, waits for them, and re-layouts: 2.33 us -> 0.01 us
  Pallas kernels: 6.99 us -> 9.01 us
    dot_general x1 -> x0, matrix products: 3.78 us -> none  [on_device(): jnp.dot(near_weights.astype(BF16), near_load, preferred_element_type=F32)]
    pallas_call x0 -> x1, Pallas kernels: none -> 3.44 us  [on_device(): call(functools.partial(host_kernel, slabs=slabs, blocks=blocks, scale=1.0...]
    ppermute x1, waiting for transfers between devices: 6.18 us -> 9.11 us  [ring(): lax.ppermute(value, axes, [(i, (i + steps) % count) for i in range(count)])]
    ppermute x1, starting transfers between devices: 3.76 us -> 1.17 us  [on_device(): cross = lax.ppermute(load, SLAB, across)]
    unnamed x6 -> x2, local copies, waits for them, and re-layouts: 2.32 us -> 0.01 us
    all_to_all x1, waiting for transfers between devices: 3.33 us -> 5.49 us  [on_device(): got = lax.all_to_all(pod_part, ROW, 0, 0, tiled=True)]
    ppermute x1, starting transfers between devices: 1.33 us -> 3.33 us  [on_device(): core = lax.ppermute(load, 'core', mates)]
    pallas_call x1, Pallas kernels: 4.44 us -> 3.02 us  [on_device(): call(functools.partial(rack_kernel, racks=racks, total=racks * shards, sl...]
  transfers between devices with their start and end apart: 8 -> 8, of which waited for: 3 -> 3; matrix products, arithmetic and copies ran while one was open for 8% -> 0% of each run, Pallas kernels for 3% -> 17%
where the time goes in v3:
time: 46 us; the launch traced here: 45.7 us
  starting transfers between devices  20.2 us (44%)
  waiting for transfers between devices  15.9 us (35%)
  Pallas kernels  9.01 us (20%)
  between operations  0.68 us (1%)
    ppermute x1, waiting for transfers between devices, ring(): lax.ppermute(value, axes, [(i, (i + steps) % count) for i in range(count)])  9.11 us
    all_to_all x1, starting transfers between devices, on_device(): got = lax.all_to_all(sent, SLAB + ('y_lo',), 0, 0, tiled=True)  6.23 us
    all_to_all x1, waiting for transfers between devices, on_device(): got = lax.all_to_all(pod_part, ROW, 0, 0, tiled=True)  5.49 us
    all_to_all x1, starting transfers between devices, on_device(): got = lax.all_to_all(pod_part, ROW, 0, 0, tiled=True)  4.86 us
    pallas_call x1, Pallas kernels, on_device(): call(functools.partial(host_kernel, slabs=slabs, blocks=blocks, scale=1.0...  3.44 us
    ppermute x1, starting transfers between devices, on_device(): core = lax.ppermute(load, 'core', mates)  3.33 us
    pallas_call x1, Pallas kernels, on_device(): call(functools.partial(rack_kernel, racks=racks, total=racks * shards, sl...  3.02 us
    ppermute x1, starting transfers between devices, on_device(): rack_cross = lax.ppermute(rack_own, SLAB, across)  1.88 us
  transfers between devices with their start and end apart: 8, of which 3 were waited for; matrix products, arithmetic and copies ran while one was open for 0% of the time, Pallas kernels for 17%

profile of v3, /device:TPU:1, one launch (start us, length us, event | category | flops | bytes accessed | tf_op | source)
XLA Modules:
  0.0 45.7 jit_solution(3704200686480658952)
XLA Ops:
  0.6 0.0 copy-start
  0.6 3.3 %collective-permute-start.1 = (bf16[72,8192]{1,0:T(8,128)(2,1)}, bf16[72,8192]{1,0:T(8,128)(2,1)S(1)}, u32[]{:S(2)}, u32[]{:S(2)}) collective-permute-start(bf16[72,8192]{1,0:T(8,128)(2,1)} %load_hbm.1), channel_id=1, source_target_pairs={{0,64},{64,0},{1,65},{65,1},{2,66},{66,2},{3,67},{67,3},{4,68},{68... | collective-permute-start | bytes 3538952 | tf_op jit(solution)/shard_map/ppermute | solution.py:191
  4.0 1.2 %collective-permute-start.2 = (bf16[72,8192]{1,0:T(8,128)(2,1)}, bf16[72,8192]{1,0:T(8,128)(2,1)S(1)}, u32[]{:S(2)}, u32[]{:S(2)}) collective-permute-start(bf16[72,8192]{1,0:T(8,128)(2,1)} %load_hbm.1), channel_id=1, source_target_pairs={{0,192},{64,128},{128,64},{192,0},{1,193},{65,129},{129,65},{193,1... | collective-permute-start | bytes 3538952 | tf_op jit(solution)/shard_map/ppermute | solution.py:190
  5.1 3.0 %rack_sums.1 = (f32[80,256]{1,0:T(8,128)S(1)}, f32[80,256]{1,0:T(8,128)S(1)}, f32[1,8192]{1,0:T(1,128)S(1)}) custom-call(s32[1]{0:T(128)} %bitcast.base_ref, s32[1]{0:T(128)} %bitcast.1.slab_ref, bf16[72,8192]{1,0:T(8,128)(2,1)} %load_hbm.1, s32[1,8192]{1,0:T(1,128)} %bitcast.6), custom_call_target="tpu_custom_call" | custom-call | flops 1 | bytes 1 | tf_op jit(solution)/shard_map/rack_sums/pallas_call | solution.py:196
  8.2 1.3 %collective-permute-start = (f32[80,256]{1,0:T(8,128)S(1)}, f32[80,256]{1,0:T(8,128)S(1)}, u32[]{:S(2)}, u32[]{:S(2)}) collective-permute-start(f32[80,256]{1,0:T(8,128)S(1)} %get-tuple-element.20), channel_id=1, source_target_pairs={{0,1},{1,2},{2,3},{3,4},{4,5},{5,6},{6,7},{7,8},{8,9},{9,10},{10,1... | collective-permute-start | bytes 245768 | tf_op jit(solution)/shard_map/ppermute | solution.py:32
  9.4 0.0 collective-permute-done.1.core_ref
  9.5 9.1 %collective-permute-done.shifted_ref = f32[80,256]{1,0:T(8,128)S(1)} collective-permute-done((f32[80,256]{1,0:T(8,128)S(1)}, f32[80,256]{1,0:T(8,128)S(1)}, u32[]{:S(2)}, u32[]{:S(2)}) %collective-permute-start) | collective-permute-done | bytes 81952 | tf_op jit(solution)/shard_map/ppermute | solution.py:32
  18.6 0.0 copy-done
  18.6 0.8 %totals.1 = (f32[32,4,128]{2,1,0:T(4,128)}, f32[72,256]{1,0:T(8,128)S(1)}, f32[1,8448]{1,0:T(1,128)S(1)}) custom-call(f32[80,256]{1,0:T(8,128)S(1)} %get-tuple-element.19.own_ref, f32[80,256]{1,0:T(8,128)S(1)} %collective-permute-done.shifted_ref, f32[1,8192]{1,0:T(1,128)S(1)} %get-tuple-element.22.far_ref, s32[1,256]{1,0:T(1,128)S(1)} %bitcast.5), custom_call_target="tpu_custom_call" | custom-call | flops 1 | bytes 1 | tf_op jit(solution)/shard_map/totals/pallas_call | solution.py:207
  19.4 4.9 %all-to-all-start = ((f32[32,4,128]{2,1,0:T(4,128)}), f32[32,4,128]{2,1,0:T(4,128)S(1)}, u32[]{:S(2)}, u32[]{:S(2)}) async-start(f32[32,4,128]{2,1,0:T(4,128)} %get-tuple-element.26), calls=%async_computation | async-start | bytes 131072 | tf_op jit(solution)/shard_map/all_to_all | solution.py:216
  24.3 1.9 %collective-permute-start.4 = (f32[72,256]{1,0:T(8,128)S(1)}, f32[72,256]{1,0:T(8,128)S(1)}, u32[]{:S(2)}, u32[]{:S(2)}) collective-permute-start(f32[72,256]{1,0:T(8,128)S(1)} %get-tuple-element.32.own_ref), channel_id=1, source_target_pairs={{0,192},{64,128},{128,64},{192,0},{1,193},{65,129},{129,65},{193,1... | collective-permute-start | bytes 221192 | tf_op jit(solution)/shard_map/ppermute | solution.py:218
  26.2 0.2 collective-permute-start.5
  26.3 1.3 %collective-permute-start.3 = (f32[1,8448]{1,0:T(1,128)S(1)}, f32[1,8448]{1,0:T(1,128)S(1)}, u32[]{:S(2)}, u32[]{:S(2)}) collective-permute-start(f32[1,8448]{1,0:T(1,128)S(1)} %get-tuple-element.28), channel_id=1, source_target_pairs={{0,128},{192,64},{1,129},{193,65},{2,130},{194,66},{3,131},{195,67... | collective-permute-start | bytes 101384 | tf_op jit(solution)/shard_map/ppermute | solution.py:219
  27.6 5.5 %all-to-all-done.got_ref = f32[32,4,128]{2,1,0:T(4,128)S(1)} async-done(((f32[32,4,128]{2,1,0:T(4,128)}), f32[32,4,128]{2,1,0:T(4,128)S(1)}, u32[]{:S(2)}, u32[]{:S(2)}) %all-to-all-start) | async-done | bytes 65568 | tf_op jit(solution)/shard_map/all_to_all | solution.py:216
  33.1 0.7 %pack.1 = f32[8,8,128]{2,1,0:T(8,128)} custom-call(f32[32,4,128]{2,1,0:T(4,128)S(1)} %all-to-all-done.got_ref), custom_call_target="tpu_custom_call" | custom-call | flops 1 | bytes 1 | tf_op jit(solution)/shard_map/pack/pallas_call | solution.py:221
  33.8 6.2 %all-to-all-start.1 = ((f32[8,8,128]{2,1,0:T(8,128)}), f32[8,8,128]{2,1,0:T(8,128)S(1)}, u32[]{:S(2)}, u32[]{:S(2)}) async-start(f32[8,8,128]{2,1,0:T(8,128)} %pack.1), calls=%async_computation.1 | async-start | bytes 65536 | tf_op jit(solution)/shard_map/all_to_all | solution.py:229
  40.0 0.0 collective-permute-done.3.far_ref
  40.0 0.0 collective-permute-done.2.cross_ref
  40.0 3.4 %host_sums.1 = f32[72,8192]{1,0:T(8,128)} custom-call(s32[1]{0:T(128)} %bitcast.1.slab_ref, bf16[72,8192]{1,0:T(8,128)(2,1)S(1)} %collective-permute-done.2.cross_ref, bf16[72,8192]{1,0:T(8,128)(2,1)} %load_hbm.1, bf16[72,8192]{1,0:T(8,128)(2,1)S(1)} %collective-permute-done.1.core_ref, f32[1,8448]{1,0:T(1,128)S(1)} %collective-permute-done.3.far_ref), custom_call_target="tpu_custom_call" | custom-call | flops 1 | bytes 1 | tf_op jit(solution)/shard_map/host_sums/pallas_call | solution.py:231
  43.4 1.2 %all-to-all-done.1.got_ref = f32[8,8,128]{2,1,0:T(8,128)S(1)} async-done(((f32[8,8,128]{2,1,0:T(8,128)}), f32[8,8,128]{2,1,0:T(8,128)S(1)}, u32[]{:S(2)}, u32[]{:S(2)}) %all-to-all-start.1) | async-done | bytes 32800 | tf_op jit(solution)/shard_map/all_to_all | solution.py:229
  44.7 0.0 collective-permute-done.4.cross_ref
  44.7 0.0 collective-permute-done.5.core_ref
  44.7 1.1 %groups.1 = (f32[72,256]{1,0:T(8,128)}, f32[2,72]{1,0:T(2,128)}) custom-call(s32[1]{0:T(128)} %bitcast.1.slab_ref, f32[8,8,128]{2,1,0:T(8,128)S(1)} %all-to-all-done.1.got_ref, f32[72,256]{1,0:T(8,128)S(1)} %collective-permute-done.4.cross_ref, f32[72,256]{1,0:T(8,128)S(1)} %get-tuple-element.32.own_ref, f32[72,256]{1,0:T(8,128)S(1)} %collective-permute-done.5.core_ref, ...), custom_call_target="tpu_custom_call" | custom-call | flops 1 | bytes 1 | tf_op jit(solution)/shard_map/groups/pallas_call | solution.py:245
Async XLA Ops:
  0.6 17.9 %copy-start = (s32[256]{0:T(256)S(1)}, s32[256]{0:T(256)}, u32[]{:S(2)}) copy-start(s32[256]{0:T(256)} %param.5) | copy-start | bytes 3076
  0.6 8.8 %collective-permute-start.1 = (bf16[72,8192]{1,0:T(8,128)(2,1)}, bf16[72,8192]{1,0:T(8,128)(2,1)S(1)}, u32[]{:S(2)}, u32[]{:S(2)}) collective-permute-start(bf16[72,8192]{1,0:T(8,128)(2,1)} %load_hbm.1), channel_id=1, source_target_pairs={{0,64},{64,0},{1,65},{65,1},{2,66},{66,2},{3,67},{67,3},{4,68},{68... | collective-permute-start | bytes 3538952 | tf_op jit(solution)/shard_map/ppermute | solution.py:191
  4.0 36.0 %collective-permute-start.2 = (bf16[72,8192]{1,0:T(8,128)(2,1)}, bf16[72,8192]{1,0:T(8,128)(2,1)S(1)}, u32[]{:S(2)}, u32[]{:S(2)}) collective-permute-start(bf16[72,8192]{1,0:T(8,128)(2,1)} %load_hbm.1), channel_id=1, source_target_pairs={{0,192},{64,128},{128,64},{192,0},{1,193},{65,129},{129,65},{193,1... | collective-permute-start | bytes 3538952 | tf_op jit(solution)/shard_map/ppermute | solution.py:190
  8.2 10.4 %collective-permute-start = (f32[80,256]{1,0:T(8,128)S(1)}, f32[80,256]{1,0:T(8,128)S(1)}, u32[]{:S(2)}, u32[]{:S(2)}) collective-permute-start(f32[80,256]{1,0:T(8,128)S(1)} %get-tuple-element.20), channel_id=1, source_target_pairs={{0,1},{1,2},{2,3},{3,4},{4,5},{5,6},{6,7},{7,8},{8,9},{9,10},{10,1... | collective-permute-start | bytes 245768 | tf_op jit(solution)/shard_map/ppermute | solution.py:32
  19.4 13.7 %all-to-all-start = ((f32[32,4,128]{2,1,0:T(4,128)}), f32[32,4,128]{2,1,0:T(4,128)S(1)}, u32[]{:S(2)}, u32[]{:S(2)}) async-start(f32[32,4,128]{2,1,0:T(4,128)} %get-tuple-element.26), calls=%async_computation | async-start | bytes 131072 | tf_op jit(solution)/shard_map/all_to_all | solution.py:216
  24.3 20.4 %collective-permute-start.4 = (f32[72,256]{1,0:T(8,128)S(1)}, f32[72,256]{1,0:T(8,128)S(1)}, u32[]{:S(2)}, u32[]{:S(2)}) collective-permute-start(f32[72,256]{1,0:T(8,128)S(1)} %get-tuple-element.32.own_ref), channel_id=1, source_target_pairs={{0,192},{64,128},{128,64},{192,0},{1,193},{65,129},{129,65},{193,1... | collective-permute-start | bytes 221192 | tf_op jit(solution)/shard_map/ppermute | solution.py:218
  26.2 18.5 %collective-permute-start.5 = (f32[72,256]{1,0:T(8,128)S(1)}, f32[72,256]{1,0:T(8,128)S(1)}, u32[]{:S(2)}, u32[]{:S(2)}) collective-permute-start(f32[72,256]{1,0:T(8,128)S(1)} %get-tuple-element.32.own_ref), channel_id=1, source_target_pairs={{0,64},{64,0},{1,65},{65,1},{2,66},{66,2},{3,67},{67,3},{4,68},{68... | collective-permute-start | bytes 221192 | tf_op jit(solution)/shard_map/ppermute | solution.py:217
  26.3 13.7 %collective-permute-start.3 = (f32[1,8448]{1,0:T(1,128)S(1)}, f32[1,8448]{1,0:T(1,128)S(1)}, u32[]{:S(2)}, u32[]{:S(2)}) collective-permute-start(f32[1,8448]{1,0:T(1,128)S(1)} %get-tuple-element.28), channel_id=1, source_target_pairs={{0,128},{192,64},{1,129},{193,65},{2,130},{194,66},{3,131},{195,67... | collective-permute-start | bytes 101384 | tf_op jit(solution)/shard_map/ppermute | solution.py:219
  33.8 10.9 %all-to-all-start.1 = ((f32[8,8,128]{2,1,0:T(8,128)}), f32[8,8,128]{2,1,0:T(8,128)S(1)}, u32[]{:S(2)}, u32[]{:S(2)}) async-start(f32[8,8,128]{2,1,0:T(8,128)} %pack.1), calls=%async_computation.1 | async-start | bytes 65536 | tf_op jit(solution)/shard_map/all_to_all | solution.py:229

commit v4 on v3

--- a/solution.py
+++ b/solution.py
@@ -188,7 +188,6 @@
     across = [(i, (i + 2 * (i % 2) - 1) % slabs) for i in range(slabs)]
     mates = [(0, 1), (1, 0)]
     cross = lax.ppermute(load, SLAB, across)
-    core = lax.ppermute(load, "core", mates)
 
     blocks = 8
     block = 4096
@@ -203,7 +202,6 @@
         out_specs=[pl.BlockSpec((tall, racks), lambda i: (0, 0))] * 2 + [pl.BlockSpec((1, block), lambda i: (0, i))],
     )(base.reshape(1), slab.reshape(1), *(pltpu.with_memory_space_constraint(x, pltpu.HBM) for x in (load, host_rack.reshape(1, hosts))))
     shifted = ring(next_part, HOST, 1)
-    far_part, core = lax.optimization_barrier((far_part, core))
     pod_part, rack_own, far_sent = call(
         functools.partial(total_kernel, per_row=row_size),
         [VMEM] * 4,
@@ -214,6 +212,7 @@
 
     later, pod_part, rack_own, far_sent = lax.optimization_barrier((load, pod_part, rack_own, far_sent))
     got = lax.all_to_all(pod_part, ROW, 0, 0, tiled=True)
+    core = lax.ppermute(later, "core", mates)
     rack_core = lax.ppermute(rack_own, "core", mates)
     rack_cross = lax.ppermute(rack_own, SLAB, across)
     far = lax.ppermute(far_sent, SLAB, [(0, 2), (3, 1)])

time: 46 us -> 44.8 us (0.974)
  waiting for transfers between devices: 15.9 us -> 12.4 us
  starting transfers between devices: 20.2 us -> 22.4 us
    ppermute x1, waiting for transfers between devices: 9.11 us -> 5.99 us  [ring(): lax.ppermute(value, axes, [(i, (i + steps) % count) for i in range(count)])]
    ppermute x1, starting transfers between devices: 1.17 us -> 3.76 us  [on_device(): cross = lax.ppermute(load, SLAB, across)]
    ppermute x1, waiting for transfers between devices: 0.01 us -> 2.17 us  [on_device(): far = lax.ppermute(far_sent, SLAB, [(0, 2), (3, 1)])]
    ppermute x1, starting transfers between devices: 3.33 us -> 1.33 us  [on_device(): core = lax.ppermute(later, 'core', mates)]
    ppermute x1, starting transfers between devices: 1.88 us -> 3.18 us  [on_device(): rack_cross = lax.ppermute(rack_own, SLAB, across)]
    all_to_all x1, waiting for transfers between devices: 5.49 us -> 4.25 us  [on_device(): got = lax.all_to_all(pod_part, ROW, 0, 0, tiled=True)]
    all_to_all x1, waiting for transfers between devices: 1.24 us -> 0.01 us  [on_device(): got = lax.all_to_all(sent, SLAB + ('y_lo',), 0, 0, tiled=True)]
    ppermute x1, starting transfers between devices: 1.29 us -> 2.12 us  [ring(): lax.ppermute(value, axes, [(i, (i + steps) % count) for i in range(count)])]
  transfers between devices with their start and end apart: 8 -> 8, of which waited for: 3 -> 3; matrix products, arithmetic and copies ran while one was open for 0% -> 0% of each run, Pallas kernels for 17% -> 11%
where the time goes in v4:
time: 44.8 us; the launch traced here: 44.5 us
  starting transfers between devices  22.4 us (50%)
  waiting for transfers between devices  12.4 us (28%)
  Pallas kernels  8.98 us (20%)
  between operations  0.71 us (2%)
    ppermute x1, waiting for transfers between devices, ring(): lax.ppermute(value, axes, [(i, (i + steps) % count) for i in range(count)])  5.99 us
    all_to_all x1, starting transfers between devices, on_device(): got = lax.all_to_all(sent, SLAB + ('y_lo',), 0, 0, tiled=True)  5.78 us
    all_to_all x1, starting transfers between devices, on_device(): got = lax.all_to_all(pod_part, ROW, 0, 0, tiled=True)  4.72 us
    all_to_all x1, waiting for transfers between devices, on_device(): got = lax.all_to_all(pod_part, ROW, 0, 0, tiled=True)  4.25 us
    ppermute x1, starting transfers between devices, on_device(): cross = lax.ppermute(load, SLAB, across)  3.76 us
    pallas_call x1, Pallas kernels, on_device(): call(functools.partial(host_kernel, slabs=slabs, blocks=blocks, scale=1.0...  3.44 us
    ppermute x1, starting transfers between devices, on_device(): rack_cross = lax.ppermute(rack_own, SLAB, across)  3.18 us
    pallas_call x1, Pallas kernels, on_device(): call(functools.partial(rack_kernel, racks=racks, total=racks * shards, sl...  3 us
  transfers between devices with their start and end apart: 8, of which 3 were waited for; matrix products, arithmetic and copies ran while one was open for 0% of the time, Pallas kernels for 11%

profile of v4, /device:TPU:1, one launch (start us, length us, event | category | flops | bytes accessed | tf_op | source)
XLA Modules:
  0.0 44.5 jit_solution(17595281777060600792)
XLA Ops:
  0.6 0.0 copy-start
  0.7 3.0 %rack_sums.1 = (f32[80,256]{1,0:T(8,128)S(1)}, f32[80,256]{1,0:T(8,128)S(1)}, f32[1,8192]{1,0:T(1,128)S(1)}) custom-call(s32[1]{0:T(128)} %bitcast.base_ref, s32[1]{0:T(128)} %bitcast.1.slab_ref, bf16[72,8192]{1,0:T(8,128)(2,1)} %load_hbm.1, s32[1,8192]{1,0:T(1,128)} %bitcast.6), custom_call_target="tpu_custom_call" | custom-call | flops 1 | bytes 1 | tf_op jit(solution)/shard_map/rack_sums/pallas_call | solution.py:195
  3.7 2.1 %collective-permute-start = (f32[80,256]{1,0:T(8,128)S(1)}, f32[80,256]{1,0:T(8,128)S(1)}, u32[]{:S(2)}, u32[]{:S(2)}) collective-permute-start(f32[80,256]{1,0:T(8,128)S(1)} %get-tuple-element.19), channel_id=1, source_target_pairs={{0,1},{1,2},{2,3},{3,4},{4,5},{5,6},{6,7},{7,8},{8,9},{9,10},{10,1... | collective-permute-start | bytes 245768 | tf_op jit(solution)/shard_map/ppermute | solution.py:32
  5.8 3.8 %collective-permute-start.1 = (bf16[72,8192]{1,0:T(8,128)(2,1)}, bf16[72,8192]{1,0:T(8,128)(2,1)S(1)}, u32[]{:S(2)}, u32[]{:S(2)}) collective-permute-start(bf16[72,8192]{1,0:T(8,128)(2,1)} %load_hbm.1), channel_id=1, source_target_pairs={{0,192},{64,128},{128,64},{192,0},{1,193},{65,129},{129,65},{193,1... | collective-permute-start | bytes 3538952 | tf_op jit(solution)/shard_map/ppermute | solution.py:190
  9.5 6.0 %collective-permute-done.shifted_ref = f32[80,256]{1,0:T(8,128)S(1)} collective-permute-done((f32[80,256]{1,0:T(8,128)S(1)}, f32[80,256]{1,0:T(8,128)S(1)}, u32[]{:S(2)}, u32[]{:S(2)}) %collective-permute-start) | collective-permute-done | bytes 81952 | tf_op jit(solution)/shard_map/ppermute | solution.py:32
  15.5 0.0 copy-done
  15.5 0.8 %totals.1 = (f32[32,4,128]{2,1,0:T(4,128)}, f32[72,256]{1,0:T(8,128)S(1)}, f32[1,8448]{1,0:T(1,128)S(1)}) custom-call(f32[80,256]{1,0:T(8,128)S(1)} %get-tuple-element.18.own_ref, f32[80,256]{1,0:T(8,128)S(1)} %collective-permute-done.shifted_ref, f32[1,8192]{1,0:T(1,128)S(1)} %get-tuple-element.20.far_ref, s32[1,256]{1,0:T(1,128)S(1)} %bitcast.5), custom_call_target="tpu_custom_call" | custom-call | flops 1 | bytes 1 | tf_op jit(solution)/shard_map/totals/pallas_call | solution.py:205
  16.4 1.3 %collective-permute-start.2 = (bf16[72,8192]{1,0:T(8,128)(2,1)}, bf16[72,8192]{1,0:T(8,128)(2,1)S(1)}, u32[]{:S(2)}, u32[]{:S(2)}) collective-permute-start(bf16[72,8192]{1,0:T(8,128)(2,1)} %load_hbm.1), channel_id=1, source_target_pairs={{0,64},{64,0},{1,65},{65,1},{2,66},{66,2},{3,67},{67,3},{4,68},{68... | collective-permute-start | bytes 3538952 | tf_op jit(solution)/shard_map/ppermute | solution.py:215
  17.7 4.7 %all-to-all-start = ((f32[32,4,128]{2,1,0:T(4,128)}), f32[32,4,128]{2,1,0:T(4,128)S(1)}, u32[]{:S(2)}, u32[]{:S(2)}) async-start(f32[32,4,128]{2,1,0:T(4,128)} %get-tuple-element.24), calls=%async_computation | async-start | bytes 131072 | tf_op jit(solution)/shard_map/all_to_all | solution.py:214
  22.4 3.2 %collective-permute-start.4 = (f32[72,256]{1,0:T(8,128)S(1)}, f32[72,256]{1,0:T(8,128)S(1)}, u32[]{:S(2)}, u32[]{:S(2)}) collective-permute-start(f32[72,256]{1,0:T(8,128)S(1)} %get-tuple-element.30.own_ref), channel_id=1, source_target_pairs={{0,192},{64,128},{128,64},{192,0},{1,193},{65,129},{129,65},{193,1... | collective-permute-start | bytes 221192 | tf_op jit(solution)/shard_map/ppermute | solution.py:217
  25.6 0.2 collective-permute-start.5
  25.8 1.3 %collective-permute-start.3 = (f32[1,8448]{1,0:T(1,128)S(1)}, f32[1,8448]{1,0:T(1,128)S(1)}, u32[]{:S(2)}, u32[]{:S(2)}) collective-permute-start(f32[1,8448]{1,0:T(1,128)S(1)} %get-tuple-element.26), channel_id=1, source_target_pairs={{0,128},{192,64},{1,129},{193,65},{2,130},{194,66},{3,131},{195,67... | collective-permute-start | bytes 101384 | tf_op jit(solution)/shard_map/ppermute | solution.py:218
  27.1 4.2 %all-to-all-done.got_ref = f32[32,4,128]{2,1,0:T(4,128)S(1)} async-done(((f32[32,4,128]{2,1,0:T(4,128)}), f32[32,4,128]{2,1,0:T(4,128)S(1)}, u32[]{:S(2)}, u32[]{:S(2)}) %all-to-all-start) | async-done | bytes 65568 | tf_op jit(solution)/shard_map/all_to_all | solution.py:214
  31.4 0.7 %pack.1 = f32[8,8,128]{2,1,0:T(8,128)} custom-call(f32[32,4,128]{2,1,0:T(4,128)S(1)} %all-to-all-done.got_ref), custom_call_target="tpu_custom_call" | custom-call | flops 1 | bytes 1 | tf_op jit(solution)/shard_map/pack/pallas_call | solution.py:220
  32.0 5.8 %all-to-all-start.1 = ((f32[8,8,128]{2,1,0:T(8,128)}), f32[8,8,128]{2,1,0:T(8,128)S(1)}, u32[]{:S(2)}, u32[]{:S(2)}) async-start(f32[8,8,128]{2,1,0:T(8,128)} %pack.1), calls=%async_computation.1 | async-start | bytes 65536 | tf_op jit(solution)/shard_map/all_to_all | solution.py:228
  37.8 2.2 %collective-permute-done.3.far_ref = f32[1,8448]{1,0:T(1,128)S(1)} collective-permute-done((f32[1,8448]{1,0:T(1,128)S(1)}, f32[1,8448]{1,0:T(1,128)S(1)}, u32[]{:S(2)}, u32[]{:S(2)}) %collective-permute-start.3) | collective-permute-done | bytes 33824 | tf_op jit(solution)/shard_map/ppermute | solution.py:218
  40.0 0.0 collective-permute-done.1.cross_ref
  40.0 0.0 collective-permute-done.2.core_ref
  40.0 3.4 %host_sums.1 = f32[72,8192]{1,0:T(8,128)} custom-call(s32[1]{0:T(128)} %bitcast.1.slab_ref, bf16[72,8192]{1,0:T(8,128)(2,1)S(1)} %collective-permute-done.1.cross_ref, bf16[72,8192]{1,0:T(8,128)(2,1)} %load_hbm.1, bf16[72,8192]{1,0:T(8,128)(2,1)S(1)} %collective-permute-done.2.core_ref, f32[1,8448]{1,0:T(1,128)S(1)} %collective-permute-done.3.far_ref), custom_call_target="tpu_custom_call" | custom-call | flops 1 | bytes 1 | tf_op jit(solution)/shard_map/host_sums/pallas_call | solution.py:230
  43.4 0.0 all-to-all-done.1.got_ref
  43.4 0.0 collective-permute-done.4.cross_ref
  43.4 0.0 collective-permute-done.5.core_ref
  43.4 1.1 %groups.1 = (f32[72,256]{1,0:T(8,128)}, f32[2,72]{1,0:T(2,128)}) custom-call(s32[1]{0:T(128)} %bitcast.1.slab_ref, f32[8,8,128]{2,1,0:T(8,128)S(1)} %all-to-all-done.1.got_ref, f32[72,256]{1,0:T(8,128)S(1)} %collective-permute-done.4.cross_ref, f32[72,256]{1,0:T(8,128)S(1)} %get-tuple-element.30.own_ref, f32[72,256]{1,0:T(8,128)S(1)} %collective-permute-done.5.core_ref, ...), custom_call_target="tpu_custom_call" | custom-call | flops 1 | bytes 1 | tf_op jit(solution)/shard_map/groups/pallas_call | solution.py:244
Async XLA Ops:
  0.6 14.9 %copy-start = (s32[256]{0:T(256)S(1)}, s32[256]{0:T(256)}, u32[]{:S(2)}) copy-start(s32[256]{0:T(256)} %param.5) | copy-start | bytes 3076
  3.7 11.9 %collective-permute-start = (f32[80,256]{1,0:T(8,128)S(1)}, f32[80,256]{1,0:T(8,128)S(1)}, u32[]{:S(2)}, u32[]{:S(2)}) collective-permute-start(f32[80,256]{1,0:T(8,128)S(1)} %get-tuple-element.19), channel_id=1, source_target_pairs={{0,1},{1,2},{2,3},{3,4},{4,5},{5,6},{6,7},{7,8},{8,9},{9,10},{10,1... | collective-permute-start | bytes 245768 | tf_op jit(solution)/shard_map/ppermute | solution.py:32
  5.8 34.2 %collective-permute-start.1 = (bf16[72,8192]{1,0:T(8,128)(2,1)}, bf16[72,8192]{1,0:T(8,128)(2,1)S(1)}, u32[]{:S(2)}, u32[]{:S(2)}) collective-permute-start(bf16[72,8192]{1,0:T(8,128)(2,1)} %load_hbm.1), channel_id=1, source_target_pairs={{0,192},{64,128},{128,64},{192,0},{1,193},{65,129},{129,65},{193,1... | collective-permute-start | bytes 3538952 | tf_op jit(solution)/shard_map/ppermute | solution.py:190
  16.4 23.6 %collective-permute-start.2 = (bf16[72,8192]{1,0:T(8,128)(2,1)}, bf16[72,8192]{1,0:T(8,128)(2,1)S(1)}, u32[]{:S(2)}, u32[]{:S(2)}) collective-permute-start(bf16[72,8192]{1,0:T(8,128)(2,1)} %load_hbm.1), channel_id=1, source_target_pairs={{0,64},{64,0},{1,65},{65,1},{2,66},{66,2},{3,67},{67,3},{4,68},{68... | collective-permute-start | bytes 3538952 | tf_op jit(solution)/shard_map/ppermute | solution.py:215
  17.7 13.7 %all-to-all-start = ((f32[32,4,128]{2,1,0:T(4,128)}), f32[32,4,128]{2,1,0:T(4,128)S(1)}, u32[]{:S(2)}, u32[]{:S(2)}) async-start(f32[32,4,128]{2,1,0:T(4,128)} %get-tuple-element.24), calls=%async_computation | async-start | bytes 131072 | tf_op jit(solution)/shard_map/all_to_all | solution.py:214
  22.4 21.0 %collective-permute-start.4 = (f32[72,256]{1,0:T(8,128)S(1)}, f32[72,256]{1,0:T(8,128)S(1)}, u32[]{:S(2)}, u32[]{:S(2)}) collective-permute-start(f32[72,256]{1,0:T(8,128)S(1)} %get-tuple-element.30.own_ref), channel_id=1, source_target_pairs={{0,192},{64,128},{128,64},{192,0},{1,193},{65,129},{129,65},{193,1... | collective-permute-start | bytes 221192 | tf_op jit(solution)/shard_map/ppermute | solution.py:217
  25.6 17.8 %collective-permute-start.5 = (f32[72,256]{1,0:T(8,128)S(1)}, f32[72,256]{1,0:T(8,128)S(1)}, u32[]{:S(2)}, u32[]{:S(2)}) collective-permute-start(f32[72,256]{1,0:T(8,128)S(1)} %get-tuple-element.30.own_ref), channel_id=1, source_target_pairs={{0,64},{64,0},{1,65},{65,1},{2,66},{66,2},{3,67},{67,3},{4,68},{68... | collective-permute-start | bytes 221192 | tf_op jit(solution)/shard_map/ppermute | solution.py:216
  25.8 14.1 %collective-permute-start.3 = (f32[1,8448]{1,0:T(1,128)S(1)}, f32[1,8448]{1,0:T(1,128)S(1)}, u32[]{:S(2)}, u32[]{:S(2)}) collective-permute-start(f32[1,8448]{1,0:T(1,128)S(1)} %get-tuple-element.26), channel_id=1, source_target_pairs={{0,128},{192,64},{1,129},{193,65},{2,130},{194,66},{3,131},{195,67... | collective-permute-start | bytes 101384 | tf_op jit(solution)/shard_map/ppermute | solution.py:218
  32.0 11.4 %all-to-all-start.1 = ((f32[8,8,128]{2,1,0:T(8,128)}), f32[8,8,128]{2,1,0:T(8,128)S(1)}, u32[]{:S(2)}, u32[]{:S(2)}) async-start(f32[8,8,128]{2,1,0:T(8,128)} %pack.1), calls=%async_computation.1 | async-start | bytes 65536 | tf_op jit(solution)/shard_map/all_to_all | solution.py:228

commit v5 on v3

--- a/solution.py
+++ b/solution.py
@@ -113,28 +113,40 @@
             out_ref[slab * lines + line] = tile
 
 
-def host_kernel(slab_ref, cross_ref, load_hbm, core_ref, far_ref, out_hbm, load_ref, out_ref, in_sems, sems, *, slabs, blocks, scale):
+def host_weights(slab, rows, slabs, turns):
+    out_step = slab * rows + lax.broadcasted_iota(I32, (rows, rows), 0)
+    step = lax.broadcasted_iota(I32, (rows, rows), 1)
+    parts = [weights(out_step, (slab + turn + slabs) % slabs * rows + step, rows * slabs) for turn in turns]
+    return jnp.concatenate([part.astype(F32) for part in parts], 1).astype(BF16)
+
+
+def chip_kernel(slab_ref, load_hbm, core_ref, sum_ref, load_ref, sems, *, slabs, blocks):
     rows, hosts = load_ref.shape
     width = hosts // blocks
     arrivals = []
     for i in range(blocks):
         part = pl.ds(i * width, width)
-        arrivals.append(pltpu.make_async_copy(load_hbm.at[:, part], load_ref.at[:, part], in_sems.at[i]))
+        arrivals.append(pltpu.make_async_copy(load_hbm.at[:, part], load_ref.at[:, part], sems.at[i]))
         arrivals[-1].start()
-    day = rows * slabs
-    slab = slab_ref[0]
-    turn = 1 - 2 * (slab % 2)
-    out_step = slab * rows + lax.broadcasted_iota(I32, (rows, rows), 0)
-    step = lax.broadcasted_iota(I32, (rows, rows), 1)
-    parts = [weights(out_step, (other + slabs) % slabs * rows + step, day) for other in (slab - turn, slab, slab + turn)]
-    matrix = jnp.concatenate([part.astype(F32) for part in parts], 1).astype(BF16)
+    slab = slab_ref[0]
+    matrix = host_weights(slab, rows, slabs, (0, 1 - 2 * (slab % 2)))
+    for i in range(blocks):
+        part = slice(i * width, (i + 1) * width)
+        arrivals[i].wait()
+        near = jnp.concatenate([load_ref[:, part], core_ref[:, part]], 0)
+        sum_ref[:, part] = lax.dot_general(matrix, near, NN, preferred_element_type=F32)
+
+
+def host_kernel(slab_ref, cross_ref, sum_ref, far_ref, out_hbm, out_ref, sems, *, slabs, blocks, scale):
+    rows, hosts = sum_ref.shape
+    width = hosts // blocks
+    slab = slab_ref[0]
+    matrix = host_weights(slab, rows, slabs, (2 * (slab % 2) - 1,))
     copies = []
     for i in range(blocks):
         part = slice(i * width, (i + 1) * width)
-        arrivals[i].wait()
-        near = jnp.concatenate([ref[:, part] for ref in (cross_ref, load_ref, core_ref)], 0)
-        sums = lax.dot_general(matrix, near, NN, preferred_element_type=F32)
-        out_ref[:, part] = (sums + far_ref[:, part]) * scale
+        sums = lax.dot_general(matrix, cross_ref[:, part], NN, preferred_element_type=F32)
+        out_ref[:, part] = (sums + sum_ref[:, part] + far_ref[:, part]) * scale
         part = pl.ds(i * width, width)
         copies.append(pltpu.make_async_copy(out_ref.at[:, part], out_hbm.at[:, part], sems.at[i]))
         copies[-1].start()
@@ -218,6 +230,14 @@
     rack_cross = lax.ppermute(rack_own, SLAB, across)
     far = lax.ppermute(far_sent, SLAB, [(0, 2), (3, 1)])
 
+    (chip_sum,) = call(
+        functools.partial(chip_kernel, slabs=slabs, blocks=blocks),
+        [SMEM, HBM, VMEM],
+        [(rows, hosts)],
+        "chip_sums",
+        out_specs=[VMEM],
+        scratch_shapes=[pltpu.VMEM((rows, hosts), BF16), pltpu.SemaphoreType.DMA((blocks,))],
+    )(slab.reshape(1), pltpu.with_memory_space_constraint(load, pltpu.HBM), core)
     (sent,) = call(
         functools.partial(pack_kernel, slabs=slabs, lines=lines),
         [VMEM],
@@ -230,17 +250,13 @@
 
     (host_drift,) = call(
         functools.partial(host_kernel, slabs=slabs, blocks=blocks, scale=1.0 / (WINDOW * math.sqrt(day))),
-        [SMEM, VMEM, HBM, VMEM, VMEM],
+        [SMEM] + [VMEM] * 3,
         [(rows, hosts)],
         "host_sums",
         out_specs=[HBM],
-        scratch_shapes=[
-            pltpu.VMEM((rows, hosts), BF16),
-            pltpu.VMEM((rows, hosts), F32),
-            pltpu.SemaphoreType.DMA((blocks,)),
-            pltpu.SemaphoreType.DMA((blocks,)),
-        ],
-    )(slab.reshape(1), cross, pltpu.with_memory_space_constraint(load, pltpu.HBM), core, far)
+        scratch_shapes=[pltpu.VMEM((rows, hosts), F32), pltpu.SemaphoreType.DMA((blocks,))],
+    )(slab.reshape(1), cross, chip_sum, far)
+
     got, host_drift = lax.optimization_barrier((got, host_drift))
     rack_drift, pod_drift = call(
         functools.partial(

time: 46 us -> 46 us (level)
  waiting for transfers between devices: 15.9 us -> 15.1 us
  Pallas kernels: 9.01 us -> 9.79 us
    pallas_call x0 -> x1, Pallas kernels: none -> 2.52 us  [on_device(): call(functools.partial(chip_kernel, slabs=slabs, blocks=blocks), [SMEM, H...]
    pallas_call x1, Pallas kernels: 3.44 us -> 1.7 us  [on_device(): call(functools.partial(host_kernel, slabs=slabs, blocks=blocks, scale=1.0...]
    all_to_all x1, waiting for transfers between devices: 1.24 us -> 0.44 us  [on_device(): got = lax.all_to_all(sent, SLAB + ('y_lo',), 0, 0, tiled=True)]
  transfers between devices with their start and end apart: 8 -> 8, of which waited for: 3 -> 3; matrix products, arithmetic and copies ran while one was open for 0% -> 0% of each run, Pallas kernels for 17% -> 19%
where the time goes in v5:
time: 46 us; the launch traced here: 45.7 us
  starting transfers between devices  20.2 us (44%)
  waiting for transfers between devices  15.1 us (33%)
  Pallas kernels  9.79 us (21%)
  between operations  0.7 us (2%)
    ppermute x1, waiting for transfers between devices, ring(): lax.ppermute(value, axes, [(i, (i + steps) % count) for i in range(count)])  9.11 us
    all_to_all x1, starting transfers between devices, on_device(): got = lax.all_to_all(sent, SLAB + ('y_lo',), 0, 0, tiled=True)  6.23 us
    all_to_all x1, waiting for transfers between devices, on_device(): got = lax.all_to_all(pod_part, ROW, 0, 0, tiled=True)  5.49 us
    all_to_all x1, starting transfers between devices, on_device(): got = lax.all_to_all(pod_part, ROW, 0, 0, tiled=True)  4.86 us
    ppermute x1, starting transfers between devices, on_device(): core = lax.ppermute(load, 'core', mates)  3.33 us
    pallas_call x1, Pallas kernels, on_device(): call(functools.partial(rack_kernel, racks=racks, total=racks * shards, sl...  3.02 us
    pallas_call x1, Pallas kernels, on_device(): call(functools.partial(chip_kernel, slabs=slabs, blocks=blocks), [SMEM, H...  2.52 us
    ppermute x1, starting transfers between devices, on_device(): rack_cross = lax.ppermute(rack_own, SLAB, across)  1.88 us
  transfers between devices with their start and end apart: 8, of which 3 were waited for; matrix products, arithmetic and copies ran while one was open for 0% of the time, Pallas kernels for 19%

profile of v5, /device:TPU:1, one launch (start us, length us, event | category | flops | bytes accessed | tf_op | source)
XLA Modules:
  0.0 45.7 jit_solution(16542527811360801557)
XLA Ops:
  0.6 0.0 copy-start
  0.6 3.3 %collective-permute-start.1 = (bf16[72,8192]{1,0:T(8,128)(2,1)}, bf16[72,8192]{1,0:T(8,128)(2,1)S(1)}, u32[]{:S(2)}, u32[]{:S(2)}) collective-permute-start(bf16[72,8192]{1,0:T(8,128)(2,1)} %load_hbm.1), channel_id=1, source_target_pairs={{0,64},{64,0},{1,65},{65,1},{2,66},{66,2},{3,67},{67,3},{4,68},{68... | collective-permute-start | bytes 3538952 | tf_op jit(solution)/shard_map/ppermute | solution.py:203
  4.0 1.2 %collective-permute-start.2 = (bf16[72,8192]{1,0:T(8,128)(2,1)}, bf16[72,8192]{1,0:T(8,128)(2,1)S(1)}, u32[]{:S(2)}, u32[]{:S(2)}) collective-permute-start(bf16[72,8192]{1,0:T(8,128)(2,1)} %load_hbm.1), channel_id=1, source_target_pairs={{0,192},{64,128},{128,64},{192,0},{1,193},{65,129},{129,65},{193,1... | collective-permute-start | bytes 3538952 | tf_op jit(solution)/shard_map/ppermute | solution.py:202
  5.1 3.0 %rack_sums.1 = (f32[80,256]{1,0:T(8,128)S(1)}, f32[80,256]{1,0:T(8,128)S(1)}, f32[1,8192]{1,0:T(1,128)S(1)}) custom-call(s32[1]{0:T(128)} %bitcast.base_ref, s32[1]{0:T(128)} %bitcast.1.slab_ref, bf16[72,8192]{1,0:T(8,128)(2,1)} %load_hbm.1, s32[1,8192]{1,0:T(1,128)} %bitcast.6), custom_call_target="tpu_custom_call" | custom-call | flops 1 | bytes 1 | tf_op jit(solution)/shard_map/rack_sums/pallas_call | solution.py:208
  8.2 1.3 %collective-permute-start = (f32[80,256]{1,0:T(8,128)S(1)}, f32[80,256]{1,0:T(8,128)S(1)}, u32[]{:S(2)}, u32[]{:S(2)}) collective-permute-start(f32[80,256]{1,0:T(8,128)S(1)} %get-tuple-element.20), channel_id=1, source_target_pairs={{0,1},{1,2},{2,3},{3,4},{4,5},{5,6},{6,7},{7,8},{8,9},{9,10},{10,1... | collective-permute-start | bytes 245768 | tf_op jit(solution)/shard_map/ppermute | solution.py:32
  9.4 0.0 collective-permute-done.1.core_ref
  9.5 9.1 %collective-permute-done.shifted_ref = f32[80,256]{1,0:T(8,128)S(1)} collective-permute-done((f32[80,256]{1,0:T(8,128)S(1)}, f32[80,256]{1,0:T(8,128)S(1)}, u32[]{:S(2)}, u32[]{:S(2)}) %collective-permute-start) | collective-permute-done | bytes 81952 | tf_op jit(solution)/shard_map/ppermute | solution.py:32
  18.6 0.0 copy-done
  18.6 0.8 %totals.1 = (f32[32,4,128]{2,1,0:T(4,128)}, f32[72,256]{1,0:T(8,128)S(1)}, f32[1,8448]{1,0:T(1,128)S(1)}) custom-call(f32[80,256]{1,0:T(8,128)S(1)} %get-tuple-element.19.own_ref, f32[80,256]{1,0:T(8,128)S(1)} %collective-permute-done.shifted_ref, f32[1,8192]{1,0:T(1,128)S(1)} %get-tuple-element.22.far_ref, s32[1,256]{1,0:T(1,128)S(1)} %bitcast.5), custom_call_target="tpu_custom_call" | custom-call | flops 1 | bytes 1 | tf_op jit(solution)/shard_map/totals/pallas_call | solution.py:219
  19.4 4.9 %all-to-all-start = ((f32[32,4,128]{2,1,0:T(4,128)}), f32[32,4,128]{2,1,0:T(4,128)S(1)}, u32[]{:S(2)}, u32[]{:S(2)}) async-start(f32[32,4,128]{2,1,0:T(4,128)} %get-tuple-element.26), calls=%async_computation | async-start | bytes 131072 | tf_op jit(solution)/shard_map/all_to_all | solution.py:228
  24.3 1.9 %collective-permute-start.4 = (f32[72,256]{1,0:T(8,128)S(1)}, f32[72,256]{1,0:T(8,128)S(1)}, u32[]{:S(2)}, u32[]{:S(2)}) collective-permute-start(f32[72,256]{1,0:T(8,128)S(1)} %get-tuple-element.32.own_ref), channel_id=1, source_target_pairs={{0,192},{64,128},{128,64},{192,0},{1,193},{65,129},{129,65},{193,1... | collective-permute-start | bytes 221192 | tf_op jit(solution)/shard_map/ppermute | solution.py:230
  26.2 0.2 collective-permute-start.5
  26.3 1.3 %collective-permute-start.3 = (f32[1,8448]{1,0:T(1,128)S(1)}, f32[1,8448]{1,0:T(1,128)S(1)}, u32[]{:S(2)}, u32[]{:S(2)}) collective-permute-start(f32[1,8448]{1,0:T(1,128)S(1)} %get-tuple-element.28), channel_id=1, source_target_pairs={{0,128},{192,64},{1,129},{193,65},{2,130},{194,66},{3,131},{195,67... | collective-permute-start | bytes 101384 | tf_op jit(solution)/shard_map/ppermute | solution.py:231
  27.6 5.5 %all-to-all-done.got_ref = f32[32,4,128]{2,1,0:T(4,128)S(1)} async-done(((f32[32,4,128]{2,1,0:T(4,128)}), f32[32,4,128]{2,1,0:T(4,128)S(1)}, u32[]{:S(2)}, u32[]{:S(2)}) %all-to-all-start) | async-done | bytes 65568 | tf_op jit(solution)/shard_map/all_to_all | solution.py:228
  33.1 0.7 %pack.1 = f32[8,8,128]{2,1,0:T(8,128)} custom-call(f32[32,4,128]{2,1,0:T(4,128)S(1)} %all-to-all-done.got_ref), custom_call_target="tpu_custom_call" | custom-call | flops 1 | bytes 1 | tf_op jit(solution)/shard_map/pack/pallas_call | solution.py:241
  33.8 6.2 %all-to-all-start.1 = ((f32[8,8,128]{2,1,0:T(8,128)}), f32[8,8,128]{2,1,0:T(8,128)S(1)}, u32[]{:S(2)}, u32[]{:S(2)}) async-start(f32[8,8,128]{2,1,0:T(8,128)} %pack.1), calls=%async_computation.1 | async-start | bytes 65536 | tf_op jit(solution)/shard_map/all_to_all | solution.py:249
  40.0 2.5 %chip_sums.1.sum_ref = f32[72,8192]{1,0:T(8,128)S(1)} custom-call(s32[1]{0:T(128)} %bitcast.1.slab_ref, bf16[72,8192]{1,0:T(8,128)(2,1)} %load_hbm.1, bf16[72,8192]{1,0:T(8,128)(2,1)S(1)} %collective-permute-done.1.core_ref), custom_call_target="tpu_custom_call" | custom-call | flops 1 | bytes 1 | tf_op jit(solution)/shard_map/chip_sums/pallas_call | solution.py:233
  42.5 0.0 collective-permute-done.3.far_ref
  42.5 0.0 collective-permute-done.2.cross_ref
  42.5 1.7 %host_sums.1 = f32[72,8192]{1,0:T(8,128)} custom-call(s32[1]{0:T(128)} %bitcast.1.slab_ref, bf16[72,8192]{1,0:T(8,128)(2,1)S(1)} %collective-permute-done.2.cross_ref, f32[72,8192]{1,0:T(8,128)S(1)} %chip_sums.1.sum_ref, f32[1,8448]{1,0:T(1,128)S(1)} %collective-permute-done.3.far_ref), custom_call_target="tpu_custom_call" | custom-call | flops 1 | bytes 1 | tf_op jit(solution)/shard_map/host_sums/pallas_call | solution.py:251
  44.2 0.4 all-to-all-done.1.got_ref
  44.7 0.0 collective-permute-done.4.cross_ref
  44.7 0.0 collective-permute-done.5.core_ref
  44.7 1.1 %groups.1 = (f32[72,256]{1,0:T(8,128)}, f32[2,72]{1,0:T(2,128)}) custom-call(s32[1]{0:T(128)} %bitcast.1.slab_ref, f32[8,8,128]{2,1,0:T(8,128)S(1)} %all-to-all-done.1.got_ref, f32[72,256]{1,0:T(8,128)S(1)} %collective-permute-done.4.cross_ref, f32[72,256]{1,0:T(8,128)S(1)} %get-tuple-element.32.own_ref, f32[72,256]{1,0:T(8,128)S(1)} %collective-permute-done.5.core_ref, ...), custom_call_target="tpu_custom_call" | custom-call | flops 1 | bytes 1 | tf_op jit(solution)/shard_map/groups/pallas_call | solution.py:261
Async XLA Ops:
  0.6 17.9 %copy-start = (s32[256]{0:T(256)S(1)}, s32[256]{0:T(256)}, u32[]{:S(2)}) copy-start(s32[256]{0:T(256)} %param.5) | copy-start | bytes 3076
  0.6 8.8 %collective-permute-start.1 = (bf16[72,8192]{1,0:T(8,128)(2,1)}, bf16[72,8192]{1,0:T(8,128)(2,1)S(1)}, u32[]{:S(2)}, u32[]{:S(2)}) collective-permute-start(bf16[72,8192]{1,0:T(8,128)(2,1)} %load_hbm.1), channel_id=1, source_target_pairs={{0,64},{64,0},{1,65},{65,1},{2,66},{66,2},{3,67},{67,3},{4,68},{68... | collective-permute-start | bytes 3538952 | tf_op jit(solution)/shard_map/ppermute | solution.py:203
  4.0 38.5 %collective-permute-start.2 = (bf16[72,8192]{1,0:T(8,128)(2,1)}, bf16[72,8192]{1,0:T(8,128)(2,1)S(1)}, u32[]{:S(2)}, u32[]{:S(2)}) collective-permute-start(bf16[72,8192]{1,0:T(8,128)(2,1)} %load_hbm.1), channel_id=1, source_target_pairs={{0,192},{64,128},{128,64},{192,0},{1,193},{65,129},{129,65},{193,1... | collective-permute-start | bytes 3538952 | tf_op jit(solution)/shard_map/ppermute | solution.py:202
  8.2 10.4 %collective-permute-start = (f32[80,256]{1,0:T(8,128)S(1)}, f32[80,256]{1,0:T(8,128)S(1)}, u32[]{:S(2)}, u32[]{:S(2)}) collective-permute-start(f32[80,256]{1,0:T(8,128)S(1)} %get-tuple-element.20), channel_id=1, source_target_pairs={{0,1},{1,2},{2,3},{3,4},{4,5},{5,6},{6,7},{7,8},{8,9},{9,10},{10,1... | collective-permute-start | bytes 245768 | tf_op jit(solution)/shard_map/ppermute | solution.py:32
  19.4 13.7 %all-to-all-start = ((f32[32,4,128]{2,1,0:T(4,128)}), f32[32,4,128]{2,1,0:T(4,128)S(1)}, u32[]{:S(2)}, u32[]{:S(2)}) async-start(f32[32,4,128]{2,1,0:T(4,128)} %get-tuple-element.26), calls=%async_computation | async-start | bytes 131072 | tf_op jit(solution)/shard_map/all_to_all | solution.py:228
  24.3 20.4 %collective-permute-start.4 = (f32[72,256]{1,0:T(8,128)S(1)}, f32[72,256]{1,0:T(8,128)S(1)}, u32[]{:S(2)}, u32[]{:S(2)}) collective-permute-start(f32[72,256]{1,0:T(8,128)S(1)} %get-tuple-element.32.own_ref), channel_id=1, source_target_pairs={{0,192},{64,128},{128,64},{192,0},{1,193},{65,129},{129,65},{193,1... | collective-permute-start | bytes 221192 | tf_op jit(solution)/shard_map/ppermute | solution.py:230
  26.2 18.5 %collective-permute-start.5 = (f32[72,256]{1,0:T(8,128)S(1)}, f32[72,256]{1,0:T(8,128)S(1)}, u32[]{:S(2)}, u32[]{:S(2)}) collective-permute-start(f32[72,256]{1,0:T(8,128)S(1)} %get-tuple-element.32.own_ref), channel_id=1, source_target_pairs={{0,64},{64,0},{1,65},{65,1},{2,66},{66,2},{3,67},{67,3},{4,68},{68... | collective-permute-start | bytes 221192 | tf_op jit(solution)/shard_map/ppermute | solution.py:229
  26.3 16.2 %collective-permute-start.3 = (f32[1,8448]{1,0:T(1,128)S(1)}, f32[1,8448]{1,0:T(1,128)S(1)}, u32[]{:S(2)}, u32[]{:S(2)}) collective-permute-start(f32[1,8448]{1,0:T(1,128)S(1)} %get-tuple-element.28), channel_id=1, source_target_pairs={{0,128},{192,64},{1,129},{193,65},{2,130},{194,66},{3,131},{195,67... | collective-permute-start | bytes 101384 | tf_op jit(solution)/shard_map/ppermute | solution.py:231
  33.8 10.9 %all-to-all-start.1 = ((f32[8,8,128]{2,1,0:T(8,128)}), f32[8,8,128]{2,1,0:T(8,128)S(1)}, u32[]{:S(2)}, u32[]{:S(2)}) async-start(f32[8,8,128]{2,1,0:T(8,128)} %pack.1), calls=%async_computation.1 | async-start | bytes 65536 | tf_op jit(solution)/shard_map/all_to_all | solution.py:249
